TPU v7x, 256 devices: a whole 4x4x8 slice. The times are simulated.
256 devices in a mesh: section: 2 (over core), row: 32 (over z, y), col: 4 (over x).
Axes of the slice: x: 4, y: 4, z: 8, core: 2. Of those that a mesh axis runs over, the one named last changes fastest.
Arguments:
- hidden_in: bfloat16 [32, 256, 3072], P('row', None, 'col')
- patch_ends: int32 [32, 4], P('row'), may hold values from 1 to 256, as said below
- timestep: int32 [32], P('row'), may hold values from 0 to 999
- mod_weight: bfloat16 [2, 256, 3, 3072], P('section'), may hold values from -0.75 to 0.75
- qkv_weight: bfloat16 [2, 3072, 3, 3072], P('section', 'row', None, 'col'), may hold values from -0.109375 to 0.109375
- out_weight: bfloat16 [2, 3072, 3072], P('section', 'col', 'row'), may hold values from -0.109375 to 0.109375
- stale_keys: bfloat16 [2, 32, 256, 3072], P('section', 'row', None, 'col'), may hold values from -1.5 to 1.5
- stale_values: bfloat16 [2, 32, 256, 3072], P('section', 'row', None, 'col'), may hold values from -6 to 6
Outputs:
- layer_out: bfloat16 [2, 32, 256, 3072], P('section', 'row', None, 'col')
Inputs may be any that keep to these rules, and one draw needn't show every extreme that they name: patch_ends rises along each request's 4 patches; each patch holds at least one and at most 64 positions, and in every draw some request has all 4 patches of exactly 64 positions.
All inputs are finite; a program needn't handle non-finite values.
Results may differ from a plain program's by a relative error of at most 0.018.
Values may be sent and summed in bfloat16 or wider, within the bound.
A program may use at most 128 MiB of HBM per device.

v0:
```python
import math

import jax
import jax.numpy as jnp
from jax import lax
from jax.sharding import PartitionSpec as P

HD = 128
FREQ = 256
NP = 4
PATCH = 64


def passed_along(array, axis, by):
    length = lax.axis_size(axis)
    pairs = [(i, i + by) for i in range(length) if 0 <= i + by < length]
    return lax.ppermute(array, axis, pairs)


def embed_time(timestep, feat_width):
    half_width = feat_width // 2
    frequency = jnp.exp(
        jnp.arange(half_width, dtype=jnp.float32) * (-math.log(10000.0) / half_width)
    )
    angles = timestep.astype(jnp.float32)[:, None] * frequency[None, :]
    return jnp.concatenate([jnp.cos(angles), jnp.sin(angles)], axis=1).astype(jnp.bfloat16)


def head_norm(raw_proj):
    shaped = raw_proj.reshape(raw_proj.shape[:-1] + (raw_proj.shape[-1] // HD, HD))
    scaled = shaped / jnp.sqrt(jnp.mean(shaped * shaped, axis=-1, keepdims=True) + 1e-06)
    return scaled.reshape(raw_proj.shape).astype(jnp.bfloat16)


def slice_one(source, first_row):
    return lax.dynamic_slice_in_dim(source, first_row, PATCH, 0)


def update_one(source, new_rows, first_row):
    return lax.dynamic_update_slice_in_dim(source, new_rows, first_row, 0)


def take_rows(source, row_begin):
    return jax.vmap(slice_one)(source, row_begin)


def put_rows(source, new_rows, row_begin, row_count, is_active):
    previous = take_rows(source, row_begin)
    keep_new = (jnp.arange(PATCH)[None, :, None] < row_count[:, None, None]) & is_active
    merged = jnp.where(keep_new, new_rows, previous)
    return jax.vmap(update_one)(source, merged, row_begin)


def attend_rows(queries, key_rows, value_rows, key_ok):
    requests = queries.shape[0]
    query_heads = queries.reshape(requests, queries.shape[1], -1, HD)
    key_heads = key_rows.reshape(requests, key_rows.shape[1], -1, HD)
    value_heads = value_rows.reshape(requests, value_rows.shape[1], -1, HD)
    scores = jnp.einsum(
        "bqhd,bkhd->bhqk", query_heads, key_heads, preferred_element_type=jnp.float32
    ) / math.sqrt(HD)
    weights = jnp.exp(scores) * key_ok[:, None, None, :]
    weights = (weights / jnp.sum(weights, axis=-1, keepdims=True)).astype(jnp.bfloat16)
    mixed = jnp.einsum("bhqk,bkhd->bqhd", weights, value_heads, preferred_element_type=jnp.float32)
    return mixed.reshape(queries.shape).astype(jnp.bfloat16)


def modulated_rows(patch_rows, shift_vec, scale_vec, col_index, col_width):
    feat_width = shift_vec.shape[-1]
    as_float = patch_rows.astype(jnp.float32)
    sum_rows, sum_squares = lax.psum(
        (jnp.sum(as_float, axis=-1), jnp.sum(as_float * as_float, axis=-1)), "col"
    )
    row_mean = (sum_rows / feat_width)[:, :, None]
    row_var = (sum_squares / feat_width)[:, :, None] - row_mean * row_mean
    shift_own = lax.dynamic_slice_in_dim(shift_vec, col_index * col_width, col_width, 1)
    scale_own = lax.dynamic_slice_in_dim(scale_vec, col_index * col_width, col_width, 1)
    normed = (as_float - row_mean) / jnp.sqrt(row_var + 1e-06)
    local_rows = (normed * (1.0 + scale_own[:, None, :]) + shift_own[:, None, :]).astype(
        jnp.bfloat16
    )
    return lax.all_gather(local_rows, "col", axis=2, tiled=True)


def shards(
    hidden_in, patch_ends, timestep, mod_weight, qkv_weight, out_weight, stale_keys, stale_values
):
    section_index = lax.axis_index("section")
    col_index = lax.axis_index("col")
    requests, slot_len, col_width = hidden_in.shape
    feat_width = mod_weight.shape[-1]
    qkv_full = lax.all_gather(qkv_weight, "row", axis=1, tiled=True)
    out_full = lax.all_gather(out_weight, "row", axis=2, tiled=True)
    qkv_matrix = qkv_full[0].reshape(feat_width, 3 * col_width)
    out_matrix = out_full[0]
    time_feats = embed_time(timestep, FREQ)
    modulation = jnp.dot(
        time_feats, mod_weight[0].reshape(FREQ, 3 * feat_width), preferred_element_type=jnp.float32
    ).reshape(requests, 3, feat_width)
    shift_vec = modulation[:, 0]
    scale_vec = modulation[:, 1]
    gate_own = lax.dynamic_slice_in_dim(modulation[:, 2], col_index * col_width, col_width, 1)
    padding = jnp.zeros((requests, PATCH, col_width), jnp.bfloat16)
    input_pad = jnp.concatenate([hidden_in, padding], axis=1)
    key_cache = jnp.concatenate([stale_keys[0], padding], axis=1)
    value_cache = jnp.concatenate([stale_values[0], padding], axis=1)
    result_pad = jnp.zeros((requests, slot_len + PATCH, col_width), jnp.bfloat16)
    patch_starts = jnp.concatenate(
        [jnp.zeros((requests, 1), jnp.int32), patch_ends[:, : NP - 1]], axis=1
    )
    seq_len = patch_ends[:, NP - 1]
    key_ok = (jnp.arange(slot_len)[None, :] < seq_len[:, None]).astype(jnp.float32)
    row_ids = jnp.arange(PATCH)
    received = padding
    for step_index in range(NP + 1):
        offset = step_index - section_index
        is_active = (offset >= 0) & (offset < NP)
        patch_index = jnp.clip(offset, 0, NP - 1)
        row_begin = jnp.take(patch_starts, patch_index, axis=1)
        row_count = jnp.take(patch_ends, patch_index, axis=1) - row_begin
        patch_rows = jnp.where(section_index == 0, take_rows(input_pad, row_begin), received)
        modulated = modulated_rows(patch_rows, shift_vec, scale_vec, col_index, col_width)
        projected = jnp.dot(
            modulated.reshape(-1, feat_width), qkv_matrix, preferred_element_type=jnp.float32
        ).reshape(requests, PATCH, 3, col_width)
        queries = head_norm(projected[:, :, 0])
        key_cache = put_rows(
            key_cache, head_norm(projected[:, :, 1]), row_begin, row_count, is_active
        )
        value_cache = put_rows(
            value_cache, projected[:, :, 2].astype(jnp.bfloat16), row_begin, row_count, is_active
        )
        attended = attend_rows(queries, key_cache[:, :slot_len], value_cache[:, :slot_len], key_ok)
        partial_out = jnp.dot(
            attended.reshape(-1, col_width), out_matrix, preferred_element_type=jnp.float32
        ).reshape(requests, PATCH, feat_width)
        summed = lax.psum_scatter(
            partial_out.astype(jnp.bfloat16), "col", scatter_dimension=2, tiled=True
        ).astype(jnp.float32)
        updated = patch_rows.astype(jnp.float32) + gate_own[:, None, :] * summed
        within = row_ids[None, :, None] < row_count[:, None, None]
        new_rows = jnp.where(within, updated, 0.0).astype(jnp.bfloat16)
        result_pad = put_rows(result_pad, new_rows, row_begin, row_count, is_active)
        if step_index < NP:
            received = passed_along(new_rows, "section", 1)
    return result_pad[None, :, :slot_len]


def solution(mesh):
    return jax.shard_map(
        shards,
        mesh=mesh,
        in_specs=(
            P("row", None, "col"),
            P("row", None),
            P("row"),
            P("section", None, None, None),
            P("section", "row", None, "col"),
            P("section", "col", "row"),
            P("section", "row", None, "col"),
            P("section", "row", None, "col"),
        ),
        out_specs=P("section", "row", None, "col"),
        check_vma=False,
    )
```

profile of v0, /device:TPU:1, one launch (start us, length us, event | category | flops | bytes accessed | tf_op | source)
XLA Modules:
  0.0 541.0 jit_solution(13146894626585429524)
XLA Ops:
  8.8 1.6 constant_dynamic-slice_fusion.8
  17.1 6.7 %copy.135 = bf16[1,256,3,3072]{1,3,2,0:T(8,128)(2,1)} copy(bf16[1,256,3,3072]{3,1,2,0:T(8,128)(2,1)} %param.41) | data formatting | bytes 9437184 | tf_op args[3]
  23.9 9.7 %all-reduce.7 = (f32[1,64]{1,0:T(1,128)S(1)}, f32[1,64]{1,0:T(1,128)S(1)}) all-reduce(f32[1,64]{1,0:T(1,128)S(1)} %bitcast.463, f32[1,64]{1,0:T(1,128)S(1)} %bitcast.462), channel_id=1, replica_groups=mesh['section'=2,'row'=32,'col'=4] {'col'}, use_global_device_ids=true, to_apply=%region_4.5 | all-reduce | flops 128 | bytes 1024 | tf_op jit(solution)/shard_map/psum | solution.py:71
  33.6 3.7 fusion.10
  40.1 4.6 and_reduce_fusion
  44.8 11.0 %all_gather.21 = bf16[1,64,3072]{2,1,0:T(8,128)(2,1)S(1)} all-gather(bf16[1,64,768]{2,1,0:T(8,128)(2,1)S(1)} %fusion.90), channel_id=1, replica_groups=mesh['section'=2,'row'=32,'col'=4] {'col'}, dimensions={2}, use_global_device_ids=true | all-gather | bytes 491520 | tf_op jit(solution)/shard_map/all_gather | solution.py:82
  55.8 85.1 %all-gather.3.cloned.1.call-done = bf16[1,3072,3,768]{3,1,2,0:T(8,128)(2,1)} async-done(((bf16[1,96,3,768]{3,1,2,0:T(8,128)(2,1)}), bf16[1,3072,3,768]{3,1,2,0:T(8,128)(2,1)}) %all-gather.3.cloned.1.call-update) | async-done | bytes 14155792 | tf_op jit(solution)/shard_map/all_gather | solution.py:92
  140.9 18.6 %copy.136 = bf16[1,3072,3,768]{1,3,2,0:T(8,128)(2,1)} copy(bf16[1,3072,3,768]{3,1,2,0:T(8,128)(2,1)} %all-gather.3.cloned.1.call-done) | data formatting | bytes 28311552 | tf_op jit(solution)/shard_map/all_gather | solution.py:92
  159.6 9.5 %fusion.52 = f32[1,64,3,768]{3,1,2,0:T(8,128)S(1)} fusion(bf16[1,3072,3,768]{1,3,2,0:T(8,128)(2,1)} %copy.136, bf16[1,64,3072]{2,1,0:T(8,128)(2,1)S(1)} %all_gather.21), kind=kOutput, calls=%fused_computation.32 | convolution fusion | flops 905969664 | bytes 15138816 | tf_op jit(solution)/shard_map/dot_general | solution.py:123
  171.7 1.4 fusion.138
  173.1 1.4 scatter.50
  174.7 1.4 scatter.51
  177.1 44.7 %all-gather.5.cloned.1.call-done = bf16[1,768,3072]{1,2,0:T(8,128)(2,1)} async-done(((bf16[1,768,96]{1,2,0:T(8,128)(2,1)}), bf16[1,768,3072]{1,2,0:T(8,128)(2,1)}) %all-gather.5.cloned.1.call-update) | async-done | bytes 4718608 | tf_op jit(solution)/shard_map/all_gather | solution.py:93
  221.8 4.6 fusion.49
  228.4 3.3 and_reduce_fusion.2
  231.7 16.2 %reduce-scatter.6.cloned.1.call-done = bf16[1,64,768]{2,1,0:T(8,128)(2,1)} async-done(((bf16[1,64,3072]{2,1,0:T(8,128)(2,1)}), bf16[1,64,768]{2,1,0:T(8,128)(2,1)}) %reduce-scatter.6.cloned.1.call-update) | async-done | bytes 98320 | tf_op jit(solution)/shard_map/reduce_scatter | solution.py:137
  247.9 1.6 select_select_fusion
  249.5 1.3 collective-permute-start
  250.8 3.5 collective-permute-done
  254.5 6.6 %all-reduce.6 = (f32[1,64]{1,0:T(1,128)S(1)}, f32[1,64]{1,0:T(1,128)S(1)}) all-reduce(f32[1,64]{1,0:T(1,128)S(1)} %bitcast.457, f32[1,64]{1,0:T(1,128)S(1)} %bitcast.456), channel_id=1, replica_groups=mesh['section'=2,'row'=32,'col'=4] {'col'}, use_global_device_ids=true, to_apply=%region_13.14 | all-reduce | flops 128 | bytes 1024 | tf_op jit(solution)/shard_map/psum | solution.py:71
  261.2 11.1 %all_gather.24 = bf16[1,64,3072]{2,1,0:T(8,128)(2,1)S(1)} all-gather(bf16[1,64,768]{2,1,0:T(8,128)(2,1)S(1)} %fusion.97), channel_id=1, replica_groups=mesh['section'=2,'row'=32,'col'=4] {'col'}, dimensions={2}, use_global_device_ids=true | all-gather | bytes 491520 | tf_op jit(solution)/shard_map/all_gather | solution.py:82
  272.3 9.4 %fusion.55 = f32[1,64,3,768]{3,1,2,0:T(8,128)S(1)} fusion(bf16[1,3072,3,768]{1,3,2,0:T(8,128)(2,1)} %copy.136, bf16[1,64,3072]{2,1,0:T(8,128)(2,1)S(1)} %all_gather.24), kind=kOutput, calls=%fused_computation.33 | convolution fusion | flops 905969664 | bytes 15138816 | tf_op jit(solution)/shard_map/dot_general | solution.py:123
  282.7 1.5 fusion.140
  284.1 1.5 scatter.56
  285.6 1.5 scatter.55
  288.3 4.6 fusion.46
  293.6 1.4 scatter.54
  295.1 22.5 %reduce-scatter.8.cloned.1.call-done = bf16[1,64,768]{2,1,0:T(8,128)(2,1)} async-done(((bf16[1,64,3072]{2,1,0:T(8,128)(2,1)}), bf16[1,64,768]{2,1,0:T(8,128)(2,1)}) %reduce-scatter.8.cloned.1.call-update) | async-done | bytes 98320 | tf_op jit(solution)/shard_map/reduce_scatter | solution.py:137
  317.5 2.3 fusion.186
  321.7 3.0 collective-permute-done.1
  324.8 6.6 %all-reduce.5 = (f32[1,64]{1,0:T(1,128)S(1)}, f32[1,64]{1,0:T(1,128)S(1)}) all-reduce(f32[1,64]{1,0:T(1,128)S(1)} %bitcast.459, f32[1,64]{1,0:T(1,128)S(1)} %bitcast.458), channel_id=1, replica_groups=mesh['section'=2,'row'=32,'col'=4] {'col'}, use_global_device_ids=true, to_apply=%region_22.23 | all-reduce | flops 128 | bytes 1024 | tf_op jit(solution)/shard_map/psum | solution.py:71
  331.5 10.9 %all_gather.25 = bf16[1,64,3072]{2,1,0:T(8,128)(2,1)S(1)} all-gather(bf16[1,64,768]{2,1,0:T(8,128)(2,1)S(1)} %fusion.104), channel_id=1, replica_groups=mesh['section'=2,'row'=32,'col'=4] {'col'}, dimensions={2}, use_global_device_ids=true | all-gather | bytes 491520 | tf_op jit(solution)/shard_map/all_gather | solution.py:82
  342.4 9.4 %fusion.58 = f32[1,64,3,768]{3,1,2,0:T(8,128)S(1)} fusion(bf16[1,3072,3,768]{1,3,2,0:T(8,128)(2,1)} %copy.136, bf16[1,64,3072]{2,1,0:T(8,128)(2,1)S(1)} %all_gather.25), kind=kOutput, calls=%fused_computation.34 | convolution fusion | flops 905969664 | bytes 15138816 | tf_op jit(solution)/shard_map/dot_general | solution.py:123
  352.8 2.0 fusion.142
  354.8 1.5 scatter.61
  356.3 1.5 scatter.60
  359.0 4.6 fusion.43
  364.4 1.5 scatter.59
  365.9 22.3 %reduce-scatter.10.cloned.1.call-done = bf16[1,64,768]{2,1,0:T(8,128)(2,1)} async-done(((bf16[1,64,3072]{2,1,0:T(8,128)(2,1)}), bf16[1,64,768]{2,1,0:T(8,128)(2,1)}) %reduce-scatter.10.cloned.1.call-update) | async-done | bytes 98320 | tf_op jit(solution)/shard_map/reduce_scatter | solution.py:137
  388.2 2.3 fusion.185
  390.5 1.5 collective-permute-start.2
  392.5 2.8 collective-permute-done.2
  395.4 6.6 %all-reduce.4 = (f32[1,64]{1,0:T(1,128)S(1)}, f32[1,64]{1,0:T(1,128)S(1)}) all-reduce(f32[1,64]{1,0:T(1,128)S(1)} %bitcast.461, f32[1,64]{1,0:T(1,128)S(1)} %bitcast.460), channel_id=1, replica_groups=mesh['section'=2,'row'=32,'col'=4] {'col'}, use_global_device_ids=true, to_apply=%region_31.32 | all-reduce | flops 128 | bytes 1024 | tf_op jit(solution)/shard_map/psum | solution.py:71
  402.2 10.9 %all_gather.26 = bf16[1,64,3072]{2,1,0:T(8,128)(2,1)S(1)} all-gather(bf16[1,64,768]{2,1,0:T(8,128)(2,1)S(1)} %fusion.111), channel_id=1, replica_groups=mesh['section'=2,'row'=32,'col'=4] {'col'}, dimensions={2}, use_global_device_ids=true | all-gather | bytes 491520 | tf_op jit(solution)/shard_map/all_gather | solution.py:82
  413.1 9.4 %fusion.61 = f32[1,64,3,768]{3,1,2,0:T(8,128)S(1)} fusion(bf16[1,3072,3,768]{1,3,2,0:T(8,128)(2,1)} %copy.136, bf16[1,64,3072]{2,1,0:T(8,128)(2,1)S(1)} %all_gather.26), kind=kOutput, calls=%fused_computation.35 | convolution fusion | flops 905969664 | bytes 15138816 | tf_op jit(solution)/shard_map/dot_general | solution.py:123
  423.5 2.0 fusion.144
  425.5 1.5 scatter.66
  427.0 1.5 scatter.65
  429.7 4.6 fusion.40
  435.0 1.5 scatter.64
  436.5 22.4 %reduce-scatter.12.cloned.1.call-done = bf16[1,64,768]{2,1,0:T(8,128)(2,1)} async-done(((bf16[1,64,3072]{2,1,0:T(8,128)(2,1)}), bf16[1,64,768]{2,1,0:T(8,128)(2,1)}) %reduce-scatter.12.cloned.1.call-update) | async-done | bytes 98320 | tf_op jit(solution)/shard_map/reduce_scatter | solution.py:137
  458.9 2.3 fusion.184
  462.5 3.5 collective-permute-done.3
  466.1 6.6 %all-reduce.3 = (f32[1,64]{1,0:T(1,128)S(1)}, f32[1,64]{1,0:T(1,128)S(1)}) all-reduce(f32[1,64]{1,0:T(1,128)S(1)} %bitcast.455, f32[1,64]{1,0:T(1,128)S(1)} %bitcast.454), channel_id=1, replica_groups=mesh['section'=2,'row'=32,'col'=4] {'col'}, use_global_device_ids=true, to_apply=%region_40.41 | all-reduce | flops 128 | bytes 1024 | tf_op jit(solution)/shard_map/psum | solution.py:71
  472.9 11.1 %all_gather.27 = bf16[1,64,3072]{2,1,0:T(8,128)(2,1)S(1)} all-gather(bf16[1,64,768]{2,1,0:T(8,128)(2,1)S(1)} %fusion.118), channel_id=1, replica_groups=mesh['section'=2,'row'=32,'col'=4] {'col'}, dimensions={2}, use_global_device_ids=true | all-gather | bytes 491520 | tf_op jit(solution)/shard_map/all_gather | solution.py:82
  484.0 9.4 %fusion.64 = f32[1,64,3,768]{3,1,2,0:T(8,128)S(1)} fusion(bf16[1,3072,3,768]{1,3,2,0:T(8,128)(2,1)} %copy.136, bf16[1,64,3072]{2,1,0:T(8,128)(2,1)S(1)} %all_gather.27), kind=kOutput, calls=%fused_computation.36 | convolution fusion | flops 905969664 | bytes 15138816 | tf_op jit(solution)/shard_map/dot_general | solution.py:123
  494.4 1.5 fusion.146
  496.0 1.5 scatter.71
  497.7 1.5 scatter.70
  500.3 4.6 fusion.37
  504.9 1.5 scatter.69
  506.4 23.0 %reduce-scatter.14.cloned.1.call-done = bf16[1,64,768]{2,1,0:T(8,128)(2,1)} async-done(((bf16[1,64,3072]{2,1,0:T(8,128)(2,1)}), bf16[1,64,768]{2,1,0:T(8,128)(2,1)}) %reduce-scatter.14.cloned.1.call-update) | async-done | bytes 98320 | tf_op jit(solution)/shard_map/reduce_scatter | solution.py:137
  529.4 2.4 fusion.163
  531.8 1.5 scatter.74
  (190 shorter events, 26.7 us)
Async XLA Ops:
  6.5 134.4 %all-gather.3.cloned.1.call-start = ((), (), s32[]{:S(2)}) async-start(), calls=%async_computation.5 | async-start | bytes 14598144 | tf_op jit(solution)/shard_map/all_gather | solution.py:92
  7.3 214.5 %all-gather.5.cloned.1.call-start = ((), (), s32[]{:S(2)}) async-start(), calls=%async_computation.6 | async-start | bytes 4866048 | tf_op jit(solution)/shard_map/all_gather | solution.py:93
  8.0 239.9 %reduce-scatter.6.cloned.1.call-start = ((), (), s32[]{:S(2)}) async-start(), calls=%async_computation.7 | async-start | bytes 491520 | tf_op jit(solution)/shard_map/reduce_scatter | solution.py:137
  17.1 6.7 %copy-start = (bf16[1,256,768]{2,1,0:T(8,128)(2,1)S(1)}, bf16[1,256,768]{2,1,0:T(8,128)(2,1)}, u32[]{:S(2)}) copy-start(bf16[1,256,768]{2,1,0:T(8,128)(2,1)} %param.38) | copy-start | bytes 1179652
  23.8 14.3 %copy-start.3 = (s32[1,2]{1,0:T(1,128)S(1)}, s32[1,2]{1,0:T(1,128)}, u32[]{:S(2)}) copy-start(s32[1,2]{1,0:T(1,128)} %constant.478.clone.1) | copy-start | bytes 28
  23.8 16.3 %copy-start.4 = (s32[3]{0:T(128)S(1)}, s32[3]{0:T(128)}, u32[]{:S(2)}) copy-start(s32[3]{0:T(128)} %constant.479.clone.1) | copy-start | bytes 40
  159.6 12.1 %copy-start.1 = (bf16[1,1,256,768]{3,2,1,0:T(8,128)(2,1)S(1)}, bf16[1,1,256,768]{3,2,1,0:T(8,128)(2,1)}, u32[]{:S(2)}) copy-start(bf16[1,1,256,768]{3,2,1,0:T(8,128)(2,1)} %param.45) | copy-start | bytes 1179652
  159.6 12.2 %copy-start.2 = (bf16[1,1,256,768]{3,2,1,0:T(8,128)(2,1)S(1)}, bf16[1,1,256,768]{3,2,1,0:T(8,128)(2,1)}, u32[]{:S(2)}) copy-start(bf16[1,1,256,768]{3,2,1,0:T(8,128)(2,1)} %param.44) | copy-start | bytes 1179652
  226.4 91.1 %reduce-scatter.8.cloned.1.call-start = ((), (), s32[]{:S(2)}) async-start(), calls=%async_computation.8 | async-start | bytes 491520 | tf_op jit(solution)/shard_map/reduce_scatter | solution.py:137
  249.5 4.8 collective-permute-start
  293.0 95.2 %reduce-scatter.10.cloned.1.call-start = ((), (), s32[]{:S(2)}) async-start(), calls=%async_computation.9 | async-start | bytes 491520 | tf_op jit(solution)/shard_map/reduce_scatter | solution.py:137
  319.9 4.8 collective-permute-start.1
  358.4 29.8 %copy-start.6 = (pred[64]{0:T(512)(128)(4,1)S(1)}, pred[64]{0:T(512)(128)(4,1)}, u32[]{:S(2)}) copy-start(pred[64]{0:T(512)(128)(4,1)} %broadcast_and_fusion.2) | copy-start | bytes 196
  363.7 95.2 %reduce-scatter.12.cloned.1.call-start = ((), (), s32[]{:S(2)}) async-start(), calls=%async_computation.10 | async-start | bytes 491520 | tf_op jit(solution)/shard_map/reduce_scatter | solution.py:137
  390.5 4.8 collective-permute-start.2
  429.1 29.8 %copy-start.5 = (pred[64]{0:T(512)(128)(4,1)S(1)}, pred[64]{0:T(512)(128)(4,1)}, u32[]{:S(2)}) copy-start(pred[64]{0:T(512)(128)(4,1)} %broadcast_and_fusion.1) | copy-start | bytes 196
  434.4 95.1 %reduce-scatter.14.cloned.1.call-start = ((), (), s32[]{:S(2)}) async-start(), calls=%async_computation.11 | async-start | bytes 491520 | tf_op jit(solution)/shard_map/reduce_scatter | solution.py:137
  461.2 4.8 collective-permute-start.3
Sparse Core Ops, SparseCore 0:
  9.9 130.9 all-gather.2
  143.5 78.2 all-gather.4
  226.5 21.3 reduce-scatter.5
  293.1 24.4 reduce-scatter.7
  363.8 24.3 reduce-scatter.9
  434.5 24.3 reduce-scatter.11
  505.0 24.3 reduce-scatter.13
where the time goes:
time: 544 us; the launch traced here: 541 us
  waiting for transfers between devices  250 us (46%)
  blocking collectives  91 us (17%)
  matrix products  76.4 us (14%)
  local copies, waits for them, and re-layouts  61.6 us (11%)
  other arithmetic  34.5 us (6%)
  between operations  21.4 us (4%)
  starting transfers between devices  5.63 us (1%)
    reduce_scatter x5, waiting for transfers between devices, shards(): lax.psum_scatter(partial_out.astype(jnp.bfloat16), 'col', scatter_dimensi...  106 us
    all_gather x1, waiting for transfers between devices, shards(): qkv_full = lax.all_gather(qkv_weight, 'row', axis=1, tiled=True)  85.1 us
    all_gather x5, blocking collectives, modulated_rows(): return lax.all_gather(local_rows, 'col', axis=2, tiled=True)  55 us
    dot_general x5, matrix products, shards(): jnp.dot(modulated.reshape(-1, feat_width), qkv_matrix, preferred_element_...  47.1 us
    all_gather x1, waiting for transfers between devices, shards(): out_full = lax.all_gather(out_weight, 'row', axis=2, tiled=True)  44.7 us
    psum x5, blocking collectives, modulated_rows(): lax.psum((jnp.sum(as_float, axis=-1), jnp.sum(as_float * as_float, axis=-...  36.1 us
    another operation x13, other arithmetic  27.2 us
    dot_general x5, matrix products, shards(): jnp.dot(attended.reshape(-1, col_width), out_matrix, preferred_element_ty...  23.1 us
  transfers between devices with their start and end apart: 11, of which 11 were waited for; matrix products, arithmetic and copies ran while one was open for 13% of the time, Pallas kernels for 0%

commit v1 on v0

v1 whole, which is shorter than its diff:
```python
import functools
import math

import jax
import jax.numpy as jnp
from jax import lax
from jax.experimental import pallas as pl
from jax.experimental.pallas import tpu as pltpu
from jax.sharding import PartitionSpec as P

HD = 128
FREQ = 256
NX, NY, NZ = 4, 4, 8
KB = 96
CW = 768
SUP = NY * KB
SLOT = 256
HEADS = CW // HD
OA = 512
OB = CW - OA
MESH = pl.DeviceIdType.MESH
F32 = jnp.float32
BF16 = jnp.bfloat16
N_SEM = 128


def embed_time(timestep):
    half_width = FREQ // 2
    frequency = jnp.exp(
        jnp.arange(half_width, dtype=F32) * (-math.log(10000.0) / half_width)
    )
    angles = timestep.astype(F32)[:, None] * frequency[None, :]
    return jnp.concatenate([jnp.cos(angles), jnp.sin(angles)], axis=1).astype(BF16)


class Links:
    def __init__(self, send_sem, recv_sem):
        self.send_sem, self.recv_sem = send_sem, recv_sem
        self.count = 0
        self.started = []

    def slot(self):
        self.count += 1
        return self.count - 1

    def copy(self, index, source, target, device):
        return pltpu.make_async_remote_copy(
            src_ref=source, dst_ref=target, send_sem=self.send_sem.at[index],
            recv_sem=self.recv_sem.at[index], device_id=device, device_id_type=MESH,
        )

    def start(self, out_view, in_view, device, target=None):
        index = self.slot()
        outgoing = self.copy(index, out_view, out_view if target is None else target, device)
        outgoing.start()
        self.started.append(outgoing)
        return self.copy(index, in_view, in_view, device)


class Gather:
    def __init__(self, links, pos, devs, views):
        self.links, self.devs = links, devs
        self.y, self.z = pos
        self.a_shard, self.a_half, self.a_sup, self.b_shard, self.b_half = views
        self.inc = {}

    def zi(self, off):
        return lax.rem(self.z + (off + NZ), NZ)

    def yi(self, off):
        return lax.rem(self.y + (off + NY), NY)

    def go(self, key, out_view, in_view, device):
        self.inc[key] = self.links.start(out_view, in_view, self.devs[device])

    def wait(self, *key):
        self.inc.pop(key).wait_recv()

    def ya_own(self):
        for sign, dev in ((1, "y+"), (-1, "y-")):
            self.go(("ya", sign), self.a_shard(self.z, self.y), self.a_shard(self.z, self.yi(-sign)), dev)

    def ya_relay(self):
        for sign, dev, half in ((1, "y+", 0), (-1, "y-", 1)):
            self.wait("ya", sign)
            self.go(("yah", sign), self.a_half(self.z, self.yi(-sign), half), self.a_half(self.z, self.yi(-2 * sign), half), dev)

    def ya_fin(self):
        for sign in (1, -1):
            self.wait("yah", sign)

    def zb_send(self, d):
        for sign, dev, half in ((1, "z+", 0), (-1, "z-", 1)):
            if d > 0:
                self.wait("zb", sign, d - 1)
            here, there = self.zi(-sign * d), self.zi(-sign * (d + 1))
            if d < NZ // 2 - 1:
                self.go(("zb", sign, d), self.b_shard(here, self.y), self.b_shard(there, self.y), dev)
            else:
                self.go(("zb", sign, d), self.b_half(here, self.y, half), self.b_half(there, self.y, half), dev)

    def zb_fin(self):
        for sign in (1, -1):
            self.wait("zb", sign, NZ // 2 - 1)

    def yb_own(self, off):
        for sign, dev in ((1, "y+"), (-1, "y-")):
            self.go(("yb", off, sign), self.b_shard(self.zi(off), self.y), self.b_shard(self.zi(off), self.yi(-sign)), dev)

    def yb_relay(self, off):
        for sign, dev, half in ((1, "y+", 0), (-1, "y-", 1)):
            self.wait("yb", off, sign)
            self.go(("ybh", off, sign), self.b_half(self.zi(off), self.yi(-sign), half), self.b_half(self.zi(off), self.yi(-2 * sign), half), dev)

    def yb_fin(self, off):
        for sign in (1, -1):
            self.wait("ybh", off, sign)

    def za_send(self, d, half):
        for sign, dev in ((1, "z+"), (-1, "z-")):
            if d == NZ // 2 - 1 and (half == 0) != (sign == 1):
                continue
            if d > 0:
                self.wait("za", sign, d - 1, half)
            here, there = self.zi(-sign * d), self.zi(-sign * (d + 1))
            self.go(("za", sign, d, half), self.a_sup(here, half), self.a_sup(there, half), dev)

    def za_fin(self):
        last = NZ // 2 - 1
        for sign, half in ((1, 1), (-1, 0)):
            self.wait("za", sign, last - 1, half)
        for sign, half in ((1, 0), (-1, 1)):
            self.wait("za", sign, last, half)


def nt_dot(left, right):
    return lax.dot_general(left, right, (((1,), (1,)), ((), ())), preferred_element_type=F32)


def kernel(
    ends_ref, feats_ref, hidden_hbm, mod_hbm, qkv_hbm, out_hbm, keys_hbm, values_hbm,
    result_ref,
    wbuf, woa, wob, modw, modv, xbuf, xm, acc, stk, stv, att, part, own_part, rs_in, res,
    send_sem, recv_sem, local_sem, gate_sem,
):
    s = lax.axis_index("section")
    row = lax.axis_index("row")
    x = lax.axis_index("col")
    z, y = row // NY, lax.rem(row, NY)

    def zy(zz, yy):
        return lax.rem(zz + NZ, NZ) * NY + lax.rem(yy + NY, NY)

    def xi(off):
        return lax.rem(x + (off + NX), NX)

    devs = {
        "y+": (s, zy(z, y + 1), x), "y-": (s, zy(z, y - 1), x),
        "z+": (s, zy(z + 1, y), x), "z-": (s, zy(z - 1, y), x),
        "x+": (s, row, xi(1)), "x-": (s, row, xi(-1)),
        "mate": (1 - s, row, x),
    }
    local = [
        pltpu.make_async_copy(qkv_hbm, wbuf.at[:, z, y], local_sem.at[0]),
        pltpu.make_async_copy(out_hbm.at[:, pl.ds(0, OA)], woa.at[z, y], local_sem.at[1]),
        pltpu.make_async_copy(out_hbm.at[:, pl.ds(OA, OB)], wob.at[z, y], local_sem.at[2]),
        pltpu.make_async_copy(mod_hbm, modw, local_sem.at[3]),
        pltpu.make_async_copy(keys_hbm, stk, local_sem.at[4]),
        pltpu.make_async_copy(values_hbm, stv, local_sem.at[5]),
    ]
    for copy in local:
        copy.start()
    load_x = pltpu.make_async_copy(hidden_hbm, xbuf.at[x], local_sem.at[6])

    @pl.when(s == 0)
    def _():
        load_x.start()

    barrier = pltpu.get_barrier_semaphore()
    for device in devs.values():
        pl.semaphore_signal(barrier, inc=1, device_id=device, device_id_type=MESH)
    pl.semaphore_wait(barrier, len(devs))

    links = Links(send_sem, recv_sem)
    qkv = Gather(links, (y, z), devs, (
        lambda zz, yy: wbuf.at[0, zz, yy],
        lambda zz, yy, h: wbuf.at[0, zz, yy, pl.ds(h * (KB // 2), KB // 2)],
        lambda zz, h: wbuf.at[0, zz, pl.ds(2 * h, 2)],
        lambda zz, yy: wbuf.at[pl.ds(1, 2), zz, yy],
        lambda zz, yy, h: wbuf.at[1 + h, zz, yy],
    ))
    out = Gather(links, (y, z), devs, (
        lambda zz, yy: woa.at[zz, yy],
        lambda zz, yy, h: woa.at[zz, yy, pl.ds(h * (KB // 2), KB // 2)],
        lambda zz, h: woa.at[zz, pl.ds(2 * h, 2)],
        lambda zz, yy: wob.at[zz, yy],
        lambda zz, yy, h: wob.at[zz, yy, pl.ds(h * (KB // 2), KB // 2)],
    ))

    handed = links.slot()
    inc = {}

    def x_start():
        @pl.when(s == 0)
        def _():
            load_x.wait()

        @pl.when(s == 1)
        def _():
            links.copy(handed, res, xbuf.at[x], devs["mate"]).wait_recv()

        for sign, dev in ((1, "x+"), (-1, "x-")):
            inc["x", sign] = links.start(xbuf.at[x], xbuf.at[xi(-sign)], devs[dev])

    def x_relay():
        half_rows = SLOT // 2
        for sign, dev, half in ((1, "x+", 0), (-1, "x-", 1)):
            rows = pl.ds(half * half_rows, half_rows)
            inc["x", sign].wait_recv()
            inc["xh", sign] = links.start(xbuf.at[xi(-sign), rows], xbuf.at[xi(-2 * sign), rows], devs[dev])

    def x_fin():
        for sign in (1, -1):
            inc["xh", sign].wait_recv()

    def modulation():
        local[3].wait()

        def body(j, _):
            modv[j] = jnp.dot(feats_ref[...], modw[j], preferred_element_type=F32)
            return 0

        lax.fori_loop(0, 3, body, 0)

    def layer_norm():
        width = NX * CW

        def body(i, _):
            rows = pl.ds(pl.multiple_of(i * 16, 16), 16)
            parts = [xbuf[c, rows, :].astype(F32) for c in range(NX)]
            total = sum(jnp.sum(p, axis=-1, keepdims=True) for p in parts)
            squares = sum(jnp.sum(p * p, axis=-1, keepdims=True) for p in parts)
            mean = total / width
            var = squares / width - mean * mean
            inv = 1.0 / jnp.sqrt(var + 1e-06)
            for b in range(NZ):
                lanes = pl.ds(b * SUP, SUP)
                piece = parts[b // 2][:, (b % 2) * SUP:(b % 2 + 1) * SUP]
                normed = (piece - mean) * inv
                xm[b, rows, :] = (normed * (1.0 + modv[1, 0:1, lanes]) + modv[0, 0:1, lanes]).astype(BF16)
            return 0

        lax.fori_loop(0, SLOT // 16, body, 0)

    def project(offs, first):
        def body(t, _):
            j = t // 3
            lanes = pl.ds(pl.multiple_of(lax.rem(t, 3) * 256, 256), 256)
            total = None
            for off in offs:
                zz = qkv.zi(off)
                block = wbuf[j, zz, :, :, lanes].reshape(SUP, 256)
                term = jnp.dot(xm[zz], block, preferred_element_type=F32)
                total = term if total is None else total + term
            if first:
                acc[j, :, lanes] = total
            else:
                acc[j, :, lanes] += total
            return 0

        lax.fori_loop(0, 9, body, 0)

    e0, e1, e2, e3 = (ends_ref[0, m] for m in range(4))
    q_pos = lax.broadcasted_iota(jnp.int32, (SLOT, 1), 0)
    limit = jnp.where(q_pos < e0, e0, jnp.where(q_pos < e1, e1, jnp.where(q_pos < e2, e2, e3)))

    def attend(first_head, heads):
        def body(h, _):
            lanes = pl.ds(pl.multiple_of(h * HD, HD), HD)
            k_pos = lax.broadcasted_iota(jnp.int32, (SLOT, SLOT), 1)
            fresh = k_pos < limit
            ok = k_pos < e3

            def norm(raw):
                return (raw * (1.0 / jnp.sqrt(jnp.mean(raw * raw, axis=-1, keepdims=True) + 1e-06))).astype(BF16)

            q = norm(acc[0, :, lanes])
            k = norm(acc[1, :, lanes])
            v = acc[2, :, lanes].astype(BF16)
            scores = jnp.where(fresh, nt_dot(q, k), nt_dot(q, stk[:, lanes])) * (1.0 / math.sqrt(HD))
            weights = jnp.where(ok, jnp.exp(scores), 0.0)
            weights = weights * (1.0 / jnp.sum(weights, axis=-1, keepdims=True))
            new_part = jnp.where(fresh, weights, 0.0).astype(BF16)
            old_part = jnp.where(fresh, 0.0, weights).astype(BF16)
            mixed = jnp.dot(new_part, v, preferred_element_type=F32) + jnp.dot(
                old_part, stv[:, lanes], preferred_element_type=F32
            )
            att[:, lanes] = mixed.astype(BF16)
            return 0

        lax.fori_loop(first_head, first_head + heads, body, 0)

    def out_block(off, store):
        owner = xi(off)
        for i in range(2):
            zz = 2 * owner + i
            term = nt_dot(att[:, 0:OA], woa[zz].reshape(SUP, OA))
            term += nt_dot(att[:, OA:CW], wob[zz].reshape(SUP, OB))
            store(slice(i * SUP, (i + 1) * SUP), term)

    def keep_part(off):
        def store(lanes, term):
            part[off, :, lanes] = term.astype(BF16)
        return store

    def keep_own(lanes, term):
        own_part[:, lanes] = term

    half_rows = SLOT // 2
    low, high = pl.ds(0, half_rows), pl.ds(half_rows, half_rows)

    def reduce_and_finish():
        first, last = (1, "x+", low, high), (-1, "x-", high, low)
        out_block(2, keep_part(2))
        opp = {}
        for sign, dev, rows, _ in (first, last):
            opp[sign] = send_part(2, rows, rs_in.at[0, rows], devs[dev])
        out_block(1, keep_part(1))
        out_block(3, keep_part(3))
        tail = []
        for sign, dev, rows, others in (first, last):
            tail.append(send_part(1 if sign == 1 else 3, others, rs_in.at[1 if sign == 1 else 2, others], devs[dev]))
        for sign, dev, rows, others in (first, last):
            opp[sign].wait_recv()
            slot = 1 if sign == 1 else 3
            part[slot, rows, :] = (part[slot, rows, :].astype(F32) + rs_in[0, rows, :].astype(F32)).astype(BF16)
            tail.append(send_part(slot, rows, rs_in.at[1 if sign == 1 else 2, rows], devs[dev]))
        out_block(0, keep_own)
        for incoming in tail:
            incoming.wait_recv()
        lanes_own = pl.ds(pl.multiple_of(x * CW, CW), CW)

        def body(i, _):
            rows = pl.ds(pl.multiple_of(i * 16, 16), 16)
            branch = own_part[rows, :] + rs_in[1, rows, :].astype(F32) + rs_in[2, rows, :].astype(F32)
            updated = xbuf[x, rows, :].astype(F32) + modv[2, 0:1, lanes_own] * branch
            pos = lax.broadcasted_iota(jnp.int32, (16, 1), 0) + i * 16
            value = jnp.where(pos < e3, updated, 0.0).astype(BF16)
            res[rows, :] = value
            return 0

        lax.fori_loop(0, SLOT // 16, body, 0)

    def send_part(slot, rows, landing, device):
        return links.start(part.at[slot, rows], landing, device, target=landing)

    local[0].wait()

    @pl.when(s == 1)
    def _():
        pl.semaphore_wait(gate_sem, 1)

    qkv.zb_send(0)
    qkv.ya_own()
    qkv.yb_own(0)
    modulation()
    qkv.ya_relay()
    qkv.zb_send(1)
    qkv.yb_own(-1)
    qkv.yb_own(1)
    qkv.yb_relay(0)
    qkv.ya_fin()
    qkv.za_send(0, 0)
    qkv.za_send(0, 1)
    qkv.zb_send(2)
    qkv.yb_own(-2)
    qkv.yb_own(2)
    qkv.yb_relay(-1)
    qkv.yb_relay(1)
    qkv.za_send(1, 0)
    qkv.za_send(1, 1)
    qkv.zb_send(3)
    qkv.yb_own(-3)
    qkv.yb_own(3)
    local[1].wait()
    local[2].wait()
    out.ya_own()
    qkv.yb_relay(-2)
    qkv.yb_relay(2)
    x_start()
    qkv.za_send(2, 0)
    qkv.za_send(2, 1)
    qkv.zb_fin()
    qkv.yb_own(4)
    out.ya_relay()
    x_relay()
    qkv.za_send(3, 0)
    qkv.za_send(3, 1)
    out.zb_send(0)
    out.ya_fin()
    out.za_send(0, 0)
    out.za_send(0, 1)
    x_fin()
    layer_norm()
    for off in (0, -1, 1, -2, 2):
        qkv.yb_fin(off)
    qkv.yb_relay(-3)
    qkv.yb_relay(3)
    out.yb_own(0)
    out.zb_send(1)
    out.yb_own(-1)
    out.yb_own(1)
    project((0, -1, 1, -2, 2), True)
    qkv.yb_relay(4)
    out.za_send(1, 0)
    out.za_send(1, 1)
    out.zb_send(2)
    out.yb_own(-2)
    out.yb_own(2)
    qkv.za_fin()
    for off in (-3, 3, 4):
        qkv.yb_fin(off)
    project((-3, 3, 4), False)
    for off in (0, -1, 1):
        out.yb_relay(off)
    out.zb_send(3)
    out.yb_own(-3)
    out.yb_own(3)
    local[4].wait()
    local[5].wait()
    attend(0, 2)
    out.za_send(2, 0)
    out.za_send(2, 1)
    out.zb_fin()
    out.yb_own(4)
    for off in (-2, 2):
        out.yb_relay(off)
    attend(2, 2)
    out.za_send(3, 0)
    out.za_send(3, 1)

    @pl.when(s == 0)
    def _():
        pl.semaphore_signal(gate_sem, inc=1, device_id=devs["mate"], device_id_type=MESH)

    for off in (-3, 3, 4):
        out.yb_relay(off)
    attend(4, 2)
    for off in (0, -1, 1, -2, 2, -3, 3, 4):
        out.yb_fin(off)
    out.za_fin()
    reduce_and_finish()

    to_mate = links.copy(handed, res, xbuf.at[x], devs["mate"])

    @pl.when(s == 0)
    def _():
        to_mate.start()

    result_ref[...] = res[...]

    @pl.when(s == 0)
    def _():
        to_mate.wait_send()

    for copy in links.started:
        copy.wait_send()


def shards(
    hidden_in, patch_ends, timestep, mod_weight, qkv_weight, out_weight, stale_keys, stale_values
):
    feats = jnp.broadcast_to(embed_time(timestep), (16, FREQ))
    mod_mat = jnp.swapaxes(mod_weight[0], 0, 1)
    qkv_mat = jnp.swapaxes(qkv_weight[0], 0, 1)
    out_mat = jnp.swapaxes(out_weight[0], 0, 1)
    anywhere = pl.BlockSpec(memory_space=pl.ANY)
    result = pl.pallas_call(
        kernel,
        out_shape=jax.ShapeDtypeStruct((SLOT, CW), BF16),
        in_specs=[
            pl.BlockSpec(memory_space=pltpu.SMEM),
            pl.BlockSpec(memory_space=pltpu.VMEM),
        ] + [anywhere] * 6,
        out_specs=pl.BlockSpec(memory_space=pltpu.VMEM),
        scratch_shapes=[
            pltpu.VMEM((3, NZ, NY, KB, CW), BF16),
            pltpu.VMEM((NZ, NY, KB, OA), BF16),
            pltpu.VMEM((NZ, NY, KB, OB), BF16),
            pltpu.VMEM((3, FREQ, NX * CW), BF16),
            pltpu.VMEM((3, 16, NX * CW), F32),
            pltpu.VMEM((NX, SLOT, CW), BF16),
            pltpu.VMEM((NZ, SLOT, SUP), BF16),
            pltpu.VMEM((3, SLOT, CW), F32),
            pltpu.VMEM((SLOT, CW), BF16),
            pltpu.VMEM((SLOT, CW), BF16),
            pltpu.VMEM((SLOT, CW), BF16),
            pltpu.VMEM((NX, SLOT, CW), BF16),
            pltpu.VMEM((SLOT, CW), F32),
            pltpu.VMEM((3, SLOT, CW), BF16),
            pltpu.VMEM((SLOT, CW), BF16),
            pltpu.SemaphoreType.DMA((N_SEM,)),
            pltpu.SemaphoreType.DMA((N_SEM,)),
            pltpu.SemaphoreType.DMA((8,)),
            pltpu.SemaphoreType.REGULAR,
        ],
        compiler_params=pltpu.CompilerParams(
            collective_id=0, has_side_effects=True, vmem_limit_bytes=62 * 1024 * 1024
        ),
        name="patch_layers",
    )(
        patch_ends, feats, hidden_in[0], mod_mat, qkv_mat, out_mat,
        stale_keys[0, 0], stale_values[0, 0],
    )
    return result[None, None]


def solution(mesh):
    return jax.shard_map(
        shards,
        mesh=mesh,
        in_specs=(
            P("row", None, "col"),
            P("row", None),
            P("row"),
            P("section", None, None, None),
            P("section", "row", None, "col"),
            P("section", "col", "row"),
            P("section", "row", None, "col"),
            P("section", "row", None, "col"),
        ),
        out_specs=P("section", "row", None, "col"),
        check_vma=False,
    )
```

time: 544 us -> 157 us (0.29)
  waiting for transfers between devices: 250 us -> 0 us
  Pallas kernels: 0 us -> 154 us
  blocking collectives: 91 us -> 0 us
  matrix products: 76.4 us -> 0 us
  local copies, waits for them, and re-layouts: 61.6 us -> 2.37 us
  other arithmetic: 34.5 us -> 0.06 us
  between operations: 21.4 us -> 0.67 us
  starting transfers between devices: 5.63 us -> 0 us
    pallas_call x0 -> x1, Pallas kernels: none -> 154 us  [shards(): pl.pallas_call(kernel, out_shape=jax.ShapeDtypeStruct((SLOT, CW), BF16),...]
    all_gather x2 -> x0, waiting for transfers between devices: 130 us -> none  [the longest x1 85.1 us: shards(): qkv_full = lax.all_gather(qkv_weight, 'row', axis=1, tiled=True)]
    reduce_scatter x5 -> x0, waiting for transfers between devices: 106 us -> none  [shards(): lax.psum_scatter(partial_out.astype(jnp.bfloat16), 'col', scatter_dimensi...]
    dot_general x21 -> x0, matrix products: 76.4 us -> none  [the longest x5 47.1 us: shards(): jnp.dot(modulated.reshape(-1, feat_width), qkv_matrix, preferred_element_...]
    all_gather x5 -> x0, blocking collectives: 55 us -> none  [modulated_rows(): return lax.all_gather(local_rows, 'col', axis=2, tiled=True)]
    psum x5 -> x0, blocking collectives: 36.1 us -> none  [modulated_rows(): lax.psum((jnp.sum(as_float, axis=-1), jnp.sum(as_float * as_float, axis=-...]
    another operation x13 -> x1, other arithmetic: 27.2 us -> 0.05 us
    scatter x15 -> x0, local copies, waits for them, and re-layouts: 22.2 us -> none  [update_one(): return lax.dynamic_update_slice_in_dim(source, new_rows, first_row, 0)]
  transfers between devices with their start and end apart: 11 -> 0, of which waited for: 11 -> 0; matrix products, arithmetic and copies ran while one was open for 13% -> 0% of each run, Pallas kernels for 0% -> 0%
where the time goes in v1:
time: 157 us
  Pallas kernels  154 us (98%)
  local copies, waits for them, and re-layouts  2.37 us (2%)
    pallas_call x1, Pallas kernels, shards(): pl.pallas_call(kernel, out_shape=jax.ShapeDtypeStruct((SLOT, CW), BF16),...  154 us

profile of v1, /device:TPU:1, one launch (start us, length us, event | category | flops | bytes accessed | tf_op | source)
XLA Modules:
  0.0 157.3 jit_solution(1564166202378540061)
XLA Ops:
  0.7 0.1 sine_convert_fusion
  0.7 0.6 broadcast_in_dim.4.feats_ref
  1.3 154.2 %patch_layers.1 = bf16[256,768]{1,0:T(8,128)(2,1)} custom-call(s32[1,4]{1,0:T(1,128)} %ends_ref.1, bf16[16,256]{1,0:T(8,128)(2,1)} %broadcast_in_dim.4.feats_ref, bf16[256,768]{1,0:T(8,128)(2,1)} %bitcast.17, bf16[3,256,3072]{2,1,0:T(8,128)(2,1)} %bitcast.14, bf16[3,96,768]{2,1,0:T(8,128)(2,1)} %bitcast.16, bf16[96,768]{1,0:T(8,128)(2,1)} %bitcast.20, ...), custom_call_target="tpu_custom_call" | custom-call | tf_op jit(solution)/shard_map/patch_layers/pallas_call | solution.py:478
  155.5 1.8 %copy.11 = bf16[1,1,256,768]{3,2,1,0:T(8,128)(2,1)} copy(bf16[1,1,256,768]{3,2,1,0:T(8,128)(2,1)} %bitcast.15) | data formatting | bytes 786432
  (1 shorter events, 0.0 us)

commit v2 on v1

--- a/solution.py
+++ b/solution.py
@@ -76,54 +76,64 @@
     def wait(self, *key):
         self.inc.pop(key).wait_recv()
 
+    def dev(self, axis, sign):
+        return axis + ("+" if sign == 1 else "-")
+
     def ya_own(self):
-        for sign, dev in ((1, "y+"), (-1, "y-")):
-            self.go(("ya", sign), self.a_shard(self.z, self.y), self.a_shard(self.z, self.yi(-sign)), dev)
-
-    def ya_relay(self):
-        for sign, dev, half in ((1, "y+", 0), (-1, "y-", 1)):
-            self.wait("ya", sign)
-            self.go(("yah", sign), self.a_half(self.z, self.yi(-sign), half), self.a_half(self.z, self.yi(-2 * sign), half), dev)
-
-    def ya_fin(self):
         for sign in (1, -1):
-            self.wait("yah", sign)
-
-    def zb_send(self, d):
-        for sign, dev, half in ((1, "z+", 0), (-1, "z-", 1)):
-            if d > 0:
-                self.wait("zb", sign, d - 1)
-            here, there = self.zi(-sign * d), self.zi(-sign * (d + 1))
-            if d < NZ // 2 - 1:
-                self.go(("zb", sign, d), self.b_shard(here, self.y), self.b_shard(there, self.y), dev)
-            else:
-                self.go(("zb", sign, d), self.b_half(here, self.y, half), self.b_half(there, self.y, half), dev)
-
-    def zb_fin(self):
+            self.go(("ya", sign), self.a_shard(self.z, self.y), self.a_shard(self.z, self.yi(-sign)), self.dev("y", sign))
+
+    def ya_relay(self, sign):
+        half = 0 if sign == 1 else 1
+        self.wait("ya", sign)
+        self.go(("yah", sign), self.a_half(self.z, self.yi(-sign), half), self.a_half(self.z, self.yi(-2 * sign), half), self.dev("y", sign))
+
+    def zb_own(self, sign):
+        self.zb_send(sign, 0)
+
+    def zb_relay(self, sign, d):
+        self.wait("zb", sign, d - 1)
+        self.zb_send(sign, d)
+
+    def zb_send(self, sign, d):
+        here, there = self.zi(-sign * d), self.zi(-sign * (d + 1))
+        if d < NZ // 2 - 1:
+            views = self.b_shard(here, self.y), self.b_shard(there, self.y)
+        else:
+            half = 0 if sign == 1 else 1
+            views = self.b_half(here, self.y, half), self.b_half(there, self.y, half)
+        self.go(("zb", sign, d), *views, self.dev("z", sign))
+
+    def yb_own(self, off):
+        if off == NZ // 2:
+            for sign in (1, -1):
+                self.wait("zb", sign, off - 1)
         for sign in (1, -1):
-            self.wait("zb", sign, NZ // 2 - 1)
-
-    def yb_own(self, off):
-        for sign, dev in ((1, "y+"), (-1, "y-")):
-            self.go(("yb", off, sign), self.b_shard(self.zi(off), self.y), self.b_shard(self.zi(off), self.yi(-sign)), dev)
-
-    def yb_relay(self, off):
-        for sign, dev, half in ((1, "y+", 0), (-1, "y-", 1)):
-            self.wait("yb", off, sign)
-            self.go(("ybh", off, sign), self.b_half(self.zi(off), self.yi(-sign), half), self.b_half(self.zi(off), self.yi(-2 * sign), half), dev)
+            self.go(("yb", off, sign), self.b_shard(self.zi(off), self.y), self.b_shard(self.zi(off), self.yi(-sign)), self.dev("y", sign))
+
+    def yb_relay(self, off, sign):
+        half = 0 if sign == 1 else 1
+        self.wait("yb", off, sign)
+        self.go(("ybh", off, sign), self.b_half(self.zi(off), self.yi(-sign), half), self.b_half(self.zi(off), self.yi(-2 * sign), half), self.dev("y", sign))
 
     def yb_fin(self, off):
         for sign in (1, -1):
             self.wait("ybh", off, sign)
 
-    def za_send(self, d, half):
-        for sign, dev in ((1, "z+"), (-1, "z-")):
-            if d == NZ // 2 - 1 and (half == 0) != (sign == 1):
-                continue
-            if d > 0:
-                self.wait("za", sign, d - 1, half)
-            here, there = self.zi(-sign * d), self.zi(-sign * (d + 1))
-            self.go(("za", sign, d, half), self.a_sup(here, half), self.a_sup(there, half), dev)
+    def za_own(self, half):
+        if half == 0:
+            for sign in (1, -1):
+                self.wait("yah", sign)
+        for sign in (1, -1):
+            self.za_send(sign, 0, half)
+
+    def za_relay(self, sign, d, half):
+        self.wait("za", sign, d - 1, half)
+        self.za_send(sign, d, half)
+
+    def za_send(self, sign, d, half):
+        here, there = self.zi(-sign * d), self.zi(-sign * (d + 1))
+        self.go(("za", sign, d, half), self.a_sup(here, half), self.a_sup(there, half), self.dev("z", sign))
 
     def za_fin(self):
         last = NZ // 2 - 1
@@ -360,94 +370,136 @@
     def _():
         pl.semaphore_wait(gate_sem, 1)
 
-    qkv.zb_send(0)
     qkv.ya_own()
-    qkv.yb_own(0)
-    modulation()
-    qkv.ya_relay()
-    qkv.zb_send(1)
-    qkv.yb_own(-1)
-    qkv.yb_own(1)
-    qkv.yb_relay(0)
-    qkv.ya_fin()
-    qkv.za_send(0, 0)
-    qkv.za_send(0, 1)
-    qkv.zb_send(2)
-    qkv.yb_own(-2)
-    qkv.yb_own(2)
-    qkv.yb_relay(-1)
-    qkv.yb_relay(1)
-    qkv.za_send(1, 0)
-    qkv.za_send(1, 1)
-    qkv.zb_send(3)
-    qkv.yb_own(-3)
-    qkv.yb_own(3)
+    qkv.zb_own(1)
+    qkv.zb_own(-1)
     local[1].wait()
     local[2].wait()
     out.ya_own()
-    qkv.yb_relay(-2)
-    qkv.yb_relay(2)
+    qkv.yb_own(0)
+    out.zb_own(1)
+    out.zb_own(-1)
+    modulation()
+    out.yb_own(0)
+    qkv.ya_relay(1)
+    qkv.ya_relay(-1)
+    out.ya_relay(1)
+    out.ya_relay(-1)
+    qkv.zb_relay(1, 1)
+    qkv.zb_relay(-1, 1)
+    qkv.yb_own(-1)
+    out.zb_relay(1, 1)
+    out.zb_relay(-1, 1)
+    qkv.yb_relay(0, 1)
+    qkv.yb_relay(0, -1)
+    qkv.za_own(0)
+    qkv.za_own(1)
+    qkv.yb_own(1)
+    qkv.zb_relay(1, 2)
+    qkv.zb_relay(-1, 2)
+    qkv.yb_relay(-1, 1)
+    qkv.yb_relay(-1, -1)
+    qkv.yb_own(-2)
+    qkv.za_relay(1, 1, 0)
+    qkv.za_relay(-1, 1, 0)
+    qkv.yb_relay(1, 1)
+    qkv.yb_relay(1, -1)
+    qkv.za_relay(1, 1, 1)
+    qkv.za_relay(-1, 1, 1)
+    qkv.yb_own(2)
+    qkv.zb_relay(1, 3)
+    qkv.zb_relay(-1, 3)
+    qkv.yb_relay(-2, 1)
+    qkv.yb_relay(-2, -1)
+    qkv.za_relay(1, 2, 0)
+    qkv.za_relay(-1, 2, 0)
+    qkv.yb_own(-3)
+    qkv.za_relay(1, 2, 1)
+    qkv.za_relay(-1, 2, 1)
+    qkv.yb_relay(2, 1)
+    qkv.yb_relay(2, -1)
+    qkv.yb_own(3)
+    out.za_own(0)
+    qkv.yb_relay(-3, 1)
+    qkv.yb_relay(-3, -1)
+    qkv.za_relay(1, 3, 0)
+    out.zb_relay(-1, 2)
     x_start()
-    qkv.za_send(2, 0)
-    qkv.za_send(2, 1)
-    qkv.zb_fin()
     qkv.yb_own(4)
-    out.ya_relay()
+    qkv.za_relay(-1, 3, 1)
+    out.zb_relay(1, 2)
+    out.za_own(1)
+    qkv.yb_relay(3, 1)
+    qkv.yb_relay(3, -1)
+    out.zb_relay(-1, 3)
+    out.za_relay(1, 1, 0)
+    out.za_relay(-1, 1, 0)
+    out.yb_relay(0, 1)
+    out.yb_relay(0, -1)
+    out.yb_own(-1)
+    out.yb_own(1)
     x_relay()
-    qkv.za_send(3, 0)
-    qkv.za_send(3, 1)
-    out.zb_send(0)
-    out.ya_fin()
-    out.za_send(0, 0)
-    out.za_send(0, 1)
+    out.yb_own(-2)
+    out.zb_relay(1, 3)
+    out.yb_own(2)
+    out.yb_own(-3)
+    qkv.yb_relay(4, 1)
+    qkv.yb_relay(4, -1)
+
+    @pl.when(s == 0)
+    def _():
+        pl.semaphore_signal(gate_sem, inc=1, device_id=devs["mate"], device_id_type=MESH)
+
+    out.za_relay(1, 1, 1)
+    out.za_relay(-1, 1, 1)
+    out.yb_own(3)
     x_fin()
     layer_norm()
-    for off in (0, -1, 1, -2, 2):
-        qkv.yb_fin(off)
-    qkv.yb_relay(-3)
-    qkv.yb_relay(3)
-    out.yb_own(0)
-    out.zb_send(1)
-    out.yb_own(-1)
-    out.yb_own(1)
+    out.yb_relay(-1, 1)
+    out.yb_relay(-1, -1)
+    out.yb_relay(1, 1)
+    out.yb_relay(1, -1)
+    out.za_relay(1, 2, 0)
+    qkv.yb_fin(0)
+    qkv.yb_fin(-1)
+    qkv.yb_fin(1)
+    qkv.yb_fin(-2)
+    qkv.yb_fin(2)
     project((0, -1, 1, -2, 2), True)
-    qkv.yb_relay(4)
-    out.za_send(1, 0)
-    out.za_send(1, 1)
-    out.zb_send(2)
-    out.yb_own(-2)
-    out.yb_own(2)
+    out.yb_relay(-2, 1)
+    out.yb_relay(-2, -1)
+    out.yb_own(4)
+    out.za_relay(-1, 2, 0)
+    out.yb_relay(2, 1)
+    out.yb_relay(2, -1)
+    out.yb_relay(-3, 1)
+    out.yb_relay(-3, -1)
+    out.za_relay(1, 2, 1)
+    out.za_relay(-1, 2, 1)
     qkv.za_fin()
-    for off in (-3, 3, 4):
-        qkv.yb_fin(off)
+    qkv.yb_fin(-3)
+    qkv.yb_fin(3)
+    qkv.yb_fin(4)
     project((-3, 3, 4), False)
-    for off in (0, -1, 1):
-        out.yb_relay(off)
-    out.zb_send(3)
-    out.yb_own(-3)
-    out.yb_own(3)
+    out.yb_relay(3, 1)
+    out.yb_relay(3, -1)
     local[4].wait()
     local[5].wait()
     attend(0, 2)
-    out.za_send(2, 0)
-    out.za_send(2, 1)
-    out.zb_fin()
-    out.yb_own(4)
-    for off in (-2, 2):
-        out.yb_relay(off)
+    out.za_relay(1, 3, 0)
+    out.yb_relay(4, 1)
+    out.yb_relay(4, -1)
     attend(2, 2)
-    out.za_send(3, 0)
-    out.za_send(3, 1)
-
-    @pl.when(s == 0)
-    def _():
-        pl.semaphore_signal(gate_sem, inc=1, device_id=devs["mate"], device_id_type=MESH)
-
-    for off in (-3, 3, 4):
-        out.yb_relay(off)
     attend(4, 2)
-    for off in (0, -1, 1, -2, 2, -3, 3, 4):
-        out.yb_fin(off)
+    out.za_relay(-1, 3, 1)
+    out.yb_fin(0)
+    out.yb_fin(-1)
+    out.yb_fin(1)
+    out.yb_fin(-2)
+    out.yb_fin(2)
+    out.yb_fin(-3)
+    out.yb_fin(3)
+    out.yb_fin(4)
     out.za_fin()
     reduce_and_finish()
 

time: 157 us -> 139 us (0.89)
  Pallas kernels: 154 us -> 136 us
    pallas_call x1, Pallas kernels: 154 us -> 136 us  [shards(): pl.pallas_call(kernel, out_shape=jax.ShapeDtypeStruct((SLOT, CW), BF16),...]
where the time goes in v2:
time: 139 us
  Pallas kernels  136 us (98%)
  local copies, waits for them, and re-layouts  2.37 us (2%)
    pallas_call x1, Pallas kernels, shards(): pl.pallas_call(kernel, out_shape=jax.ShapeDtypeStruct((SLOT, CW), BF16),...  136 us

profile of v2, /device:TPU:1, one launch (start us, length us, event | category | flops | bytes accessed | tf_op | source)
XLA Modules:
  0.0 139.3 jit_solution(16954238638764822537)
XLA Ops:
  0.7 0.1 sine_convert_fusion
  0.7 0.6 broadcast_in_dim.4.feats_ref
  1.3 136.1 %patch_layers.1 = bf16[256,768]{1,0:T(8,128)(2,1)} custom-call(s32[1,4]{1,0:T(1,128)} %ends_ref.1, bf16[16,256]{1,0:T(8,128)(2,1)} %broadcast_in_dim.4.feats_ref, bf16[256,768]{1,0:T(8,128)(2,1)} %bitcast.17, bf16[3,256,3072]{2,1,0:T(8,128)(2,1)} %bitcast.14, bf16[3,96,768]{2,1,0:T(8,128)(2,1)} %bitcast.16, bf16[96,768]{1,0:T(8,128)(2,1)} %bitcast.20, ...), custom_call_target="tpu_custom_call" | custom-call | tf_op jit(solution)/shard_map/patch_layers/pallas_call | solution.py:530
  137.5 1.8 %copy.11 = bf16[1,1,256,768]{3,2,1,0:T(8,128)(2,1)} copy(bf16[1,1,256,768]{3,2,1,0:T(8,128)(2,1)} %bitcast.15) | data formatting | bytes 786432
  (1 shorter events, 0.0 us)

commit v3 on v0

v3 whole, which is shorter than its diff:
```python
import functools
import math

import jax
import jax.numpy as jnp
from jax import lax
from jax.experimental import pallas as pl
from jax.experimental.pallas import tpu as pltpu
from jax.sharding import PartitionSpec as P

HD = 128
FREQ = 256
NX, NY, NZ = 4, 4, 8
KB = 96
CW = 768
SUP = NY * KB
SLOT = 256
HEADS = CW // HD
OA = 512
OB = CW - OA
OA2, OB2 = OA // 2, OB // 2
MESH = pl.DeviceIdType.MESH
F32 = jnp.float32
BF16 = jnp.bfloat16
N_SEM = 160


def embed_time(timestep):
    half_width = FREQ // 2
    frequency = jnp.exp(
        jnp.arange(half_width, dtype=F32) * (-math.log(10000.0) / half_width)
    )
    angles = timestep.astype(F32)[:, None] * frequency[None, :]
    return jnp.concatenate([jnp.cos(angles), jnp.sin(angles)], axis=1).astype(BF16)


class Links:
    def __init__(self, send_sem, recv_sem):
        self.send_sem, self.recv_sem = send_sem, recv_sem
        self.count = 0
        self.started = []

    def slot(self):
        self.count += 1
        return self.count - 1

    def copy(self, index, source, target, device):
        return pltpu.make_async_remote_copy(
            src_ref=source, dst_ref=target, send_sem=self.send_sem.at[index],
            recv_sem=self.recv_sem.at[index], device_id=device, device_id_type=MESH,
        )

    def start(self, out_view, in_view, device, target=None):
        index = self.slot()
        outgoing = self.copy(index, out_view, out_view if target is None else target, device)
        outgoing.start()
        self.started.append(outgoing)
        return self.copy(index, in_view, in_view, device)


class Gather:
    def __init__(self, links, pos, devs, views):
        self.links, self.devs = links, devs
        self.y, self.z = pos
        self.a_shard, self.a_half, self.a_sup, self.b_shard, self.b_half = views
        self.inc = {}

    def zi(self, off):
        return lax.rem(self.z + (off + NZ), NZ)

    def yi(self, off):
        return lax.rem(self.y + (off + NY), NY)

    def go(self, key, out_view, in_view, device):
        self.inc[key] = self.links.start(out_view, in_view, self.devs[device])

    def wait(self, *key):
        self.inc.pop(key).wait_recv()

    def dev(self, axis, sign):
        return axis + ("+" if sign == 1 else "-")

    def ya_own(self):
        for sign in (1, -1):
            self.go(("ya", sign), self.a_shard(self.z, self.y), self.a_shard(self.z, self.yi(-sign)), self.dev("y", sign))

    def ya_relay(self, sign):
        half = 0 if sign == 1 else 1
        self.wait("ya", sign)
        self.go(("yah", sign), self.a_half(self.z, self.yi(-sign), half), self.a_half(self.z, self.yi(-2 * sign), half), self.dev("y", sign))

    def zb_own(self, sign):
        self.zb_send(sign, 0)

    def zb_relay(self, sign, d):
        self.wait("zb", sign, d - 1)
        self.zb_send(sign, d)

    def zb_send(self, sign, d):
        here, there = self.zi(-sign * d), self.zi(-sign * (d + 1))
        if d < NZ // 2 - 1:
            views = self.b_shard(here, self.y), self.b_shard(there, self.y)
        else:
            half = 0 if sign == 1 else 1
            views = self.b_half(here, self.y, half), self.b_half(there, self.y, half)
        self.go(("zb", sign, d), *views, self.dev("z", sign))

    def yb_own(self, off):
        if off == NZ // 2:
            for sign in (1, -1):
                self.wait("zb", sign, off - 1)
        for sign in (1, -1):
            self.go(("yb", off, sign), self.b_shard(self.zi(off), self.y), self.b_shard(self.zi(off), self.yi(-sign)), self.dev("y", sign))

    def yb_relay(self, off, sign):
        half = 0 if sign == 1 else 1
        self.wait("yb", off, sign)
        self.go(("ybh", off, sign), self.b_half(self.zi(off), self.yi(-sign), half), self.b_half(self.zi(off), self.yi(-2 * sign), half), self.dev("y", sign))

    def za_own(self, half):
        if half == 0:
            for sign in (1, -1):
                self.wait("yah", sign)
        for sign in (1, -1):
            self.za_send(sign, 0, half)

    def za_relay(self, sign, d, half):
        self.wait("za", sign, d - 1, half)
        self.za_send(sign, d, half)

    def za_send(self, sign, d, half):
        here, there = self.zi(-sign * d), self.zi(-sign * (d + 1))
        self.go(("za", sign, d, half), self.a_sup(here, half), self.a_sup(there, half), self.dev("z", sign))

    def fin(self, off):
        for sign in (1, -1):
            self.wait("ybh", off, sign)
        for key in [k for k in self.inc if k[0] == "za" and -k[1] * (k[2] + 1) % NZ == off % NZ]:
            self.wait(*key)


class PairGather:
    def __init__(self, links, pos, devs, views):
        self.links, self.devs = links, devs
        self.y, self.z = pos
        self.mate_y = NY - 1 - self.y
        self.near_y = self.y + 1 - 2 * lax.rem(self.y, 2)
        self.source, self.landing, self.a_slot, self.a_sup, self.b_slot = views
        self.inc = {}

    def zi(self, off):
        return lax.rem(self.z + (off + NZ), NZ)

    def slot(self, k):
        return self.y if k == 0 else self.mate_y

    def near_slot(self, k):
        return self.near_y if k == 0 else NY - 1 - self.near_y

    def go(self, key, out_view, in_view, device, target=None):
        self.inc[key] = self.links.start(out_view, in_view, self.devs[device], target)

    def wait(self, *key):
        self.inc.pop(key).wait_recv()

    def inject(self):
        for i, (source, target) in enumerate(zip(self.source, self.landing(self.y))):
            self.go(("inj", i), source, self.landing(self.mate_y)[i], "pair", target)

    def injected(self):
        for i in range(len(self.source)):
            if ("inj", i) in self.inc:
                self.wait("inj", i)

    def ya_own(self, k):
        if k == 1:
            self.injected()
        self.go(("ya", k), self.a_slot(self.z, self.slot(k)), self.a_slot(self.z, self.near_slot(k)), "near")

    def za_own(self, half):
        if half == 0:
            for k in range(2):
                self.wait("ya", k)
        for sign in (1, -1):
            self.za_send(sign, 0, half)

    def za_relay(self, sign, d, half):
        self.wait("za", sign, d - 1, half)
        self.za_send(sign, d, half)

    def za_send(self, sign, d, half):
        here, there = self.zi(-sign * d), self.zi(-sign * (d + 1))
        self.go(("za", sign, d, half), self.a_sup(here, half), self.a_sup(there, half), "z+" if sign == 1 else "z-")

    def zb_own(self, k, sign):
        if k == 1:
            self.injected()
        self.zb_send(k, sign, 0)

    def zb_relay(self, k, sign, d):
        self.wait("zb", k, sign, d - 1)
        self.zb_send(k, sign, d)

    def zb_send(self, k, sign, d):
        here, there = self.zi(-sign * d), self.zi(-sign * (d + 1))
        self.go(("zb", k, sign, d), self.b_slot(here, self.slot(k)), self.b_slot(there, self.slot(k)), "z+" if sign == 1 else "z-")

    def yb_own(self, off, k):
        if off == 0 and k == 1:
            self.injected()
        for sign in (1, -1):
            for d in range(NZ // 2):
                if off % NZ == -sign * (d + 1) % NZ and ("zb", k, sign, d) in self.inc:
                    self.wait("zb", k, sign, d)
        self.go(("yb", off, k), self.b_slot(self.zi(off), self.slot(k)), self.b_slot(self.zi(off), self.near_slot(k)), "near")

    def fin(self, off):
        for k in range(2):
            self.wait("yb", off, k)
        self.fin_a(off)

    def fin_a(self, off):
        for key in [k for k in self.inc if k[0] == "za" and -k[1] * (k[2] + 1) % NZ == off % NZ]:
            self.wait(*key)


def nt_dot(left, right):
    return lax.dot_general(left, right, (((1,), (1,)), ((), ())), preferred_element_type=F32)


def kernel(
    ends_ref, feats_ref, marks_ref, hidden_hbm, mod_hbm, qkv_hbm, out_hbm, keys_hbm, values_hbm,
    result_ref,
    wbuf, woa, wob, modw, modv, xbuf, xm, acc, acc2, stk, stv, stk2, stv2, att, att2, part, own_part, rs_in, pair_in,
    feats_in, marks, res,
    send_sem, recv_sem, local_sem, hand_sem, gate_sem,
):
    s = lax.axis_index("section")
    row = lax.axis_index("row")
    x = lax.axis_index("col")
    z, y = row // NY, lax.rem(row, NY)

    def zy(zz, yy):
        return lax.rem(zz + NZ, NZ) * NY + lax.rem(yy + NY, NY)

    def xi(off):
        return lax.rem(x + (off + NX), NX)

    devs = {
        "y+": (s, zy(z, y + 1), x), "y-": (s, zy(z, y - 1), x),
        "z+": (s, zy(z + 1, y), x), "z-": (s, zy(z - 1, y), x),
        "x+": (s, row, xi(1)), "x-": (s, row, xi(-1)),
        "mate": (1 - s, row, x),
    }
    load_mod = pltpu.make_async_copy(mod_hbm, modw, local_sem.at[3])
    load_mod.start()
    load_x = pltpu.make_async_copy(hidden_hbm, xbuf.at[0, x], local_sem.at[6])
    half_lanes = CW // 2
    group = y // 2
    mine = pl.ds(pl.multiple_of(group * half_lanes, half_lanes), half_lanes)
    other = pl.ds(pl.multiple_of((1 - group) * half_lanes, half_lanes), half_lanes)

    def out_lanes(which, size, start):
        return pl.ds(pl.multiple_of(which * half_lanes + start, HD), size)

    whole = [
        pltpu.make_async_copy(qkv_hbm, wbuf.at[:, z, y], local_sem.at[0]),
        pltpu.make_async_copy(out_hbm.at[:, pl.ds(0, OA)], woa.at[z, y], local_sem.at[1]),
        pltpu.make_async_copy(out_hbm.at[:, pl.ds(OA, OB)], wob.at[z, y], local_sem.at[2]),
        pltpu.make_async_copy(keys_hbm, stk, local_sem.at[4]),
        pltpu.make_async_copy(values_hbm, stv, local_sem.at[5]),
    ]
    halves = [
        pltpu.make_async_copy(qkv_hbm.at[:, :, mine], wbuf.at[:, z, y, :, pl.ds(0, half_lanes)], local_sem.at[0]),
        pltpu.make_async_copy(out_hbm.at[:, out_lanes(group, OA2, 0)], woa.at[z, y, :, pl.ds(0, OA2)], local_sem.at[1]),
        pltpu.make_async_copy(out_hbm.at[:, out_lanes(group, OB2, OA2)], wob.at[z, y, :, pl.ds(0, OB2)], local_sem.at[2]),
        pltpu.make_async_copy(keys_hbm.at[:, mine], stk2.at[0], local_sem.at[4]),
        pltpu.make_async_copy(values_hbm.at[:, mine], stv2.at[0], local_sem.at[5]),
    ]

    @pl.when(s == 0)
    def _():
        for copy in halves:
            copy.start()
        load_x.start()

    @pl.when(s == 1)
    def _():
        for copy in whole:
            copy.start()

    marks[0] = marks_ref[...]

    barrier = pltpu.get_barrier_semaphore()
    for device in devs.values():
        pl.semaphore_signal(barrier, inc=1, device_id=device, device_id_type=MESH)
    pl.semaphore_wait(barrier, len(devs))

    handed = pltpu.make_async_remote_copy(
        src_ref=res, dst_ref=xbuf.at[0, x], send_sem=hand_sem.at[0], recv_sem=hand_sem.at[1],
        device_id=devs["mate"], device_id_type=MESH,
    )

    def modulation(r, feats):
        def body(j, _):
            modv[r, j] = jnp.dot(feats[...], modw[j], preferred_element_type=F32)
            return 0

        lax.fori_loop(0, 3, body, 0)

    def layer_norm(first, count):
        width = NX * CW

        def body(i, _):
            r = first * 64 // SLOT
            rows = pl.ds(pl.multiple_of(i * 16 - r * SLOT, 16), 16)
            to_rows = pl.ds(pl.multiple_of(i * 16, 16), 16)
            parts = [xbuf[r, c, rows, :].astype(F32) for c in range(NX)]
            total = sum(jnp.sum(p, axis=-1, keepdims=True) for p in parts)
            squares = sum(jnp.sum(p * p, axis=-1, keepdims=True) for p in parts)
            mean = total / width
            var = squares / width - mean * mean
            inv = 1.0 / jnp.sqrt(var + 1e-06)
            for b in range(NZ):
                lanes = pl.ds(b * SUP, SUP)
                piece = parts[b // 2][:, (b % 2) * SUP:(b % 2 + 1) * SUP]
                normed = (piece - mean) * inv
                xm[b, to_rows, :] = (normed * (1.0 + modv[r, 1, 0:1, lanes]) + modv[r, 0, 0:1, lanes]).astype(BF16)
            return 0

        lax.fori_loop(first * 4, (first + count) * 4, body, 0)

    def attend_head(q, k, v, old_k, old_v, mark):
        e0, e1, e2, e3 = (mark[0:1, m:m + 1] for m in range(4))
        q_pos = lax.broadcasted_iota(jnp.int32, (SLOT, 1), 0)
        limit = jnp.where(q_pos < e0, e0, jnp.where(q_pos < e1, e1, jnp.where(q_pos < e2, e2, e3)))
        k_pos = lax.broadcasted_iota(jnp.int32, (SLOT, SLOT), 1)
        fresh = k_pos < limit
        ok = k_pos < e3

        def norm(raw):
            return (raw * (1.0 / jnp.sqrt(jnp.mean(raw * raw, axis=-1, keepdims=True) + 1e-06))).astype(BF16)

        q, k, v = norm(q), norm(k), v.astype(BF16)
        scores = jnp.where(fresh, nt_dot(q, k), nt_dot(q, old_k)) * (1.0 / math.sqrt(HD))
        weights = jnp.where(ok, jnp.exp(scores), 0.0)
        weights = weights * (1.0 / jnp.sum(weights, axis=-1, keepdims=True))
        new_part = jnp.where(fresh, weights, 0.0).astype(BF16)
        old_part = jnp.where(fresh, 0.0, weights).astype(BF16)
        mixed = jnp.dot(new_part, v, preferred_element_type=F32) + jnp.dot(
            old_part, old_v, preferred_element_type=F32
        )
        return mixed.astype(BF16)

    e3 = ends_ref[0, 3]
    half_rows = SLOT // 2
    lanes_own = pl.ds(pl.multiple_of(x * CW, CW), CW)

    class Summed:
        def __init__(self, links, base, block):
            self.links, self.base, self.block = links, base, block
            self.low, self.high = pl.ds(base, half_rows), pl.ds(base + half_rows, half_rows)
            self.ways = ((1, "x+", self.low, self.high, 1), (-1, "x-", self.high, self.low, 3))
            self.opp, self.tail = {}, []

        def rows(self):
            return pl.ds(self.base, SLOT)

        def term(self, off):
            for i in range(2):
                value = self.block(2 * xi(off) + i)
                if off == 0:
                    own_part[self.rows(), i * SUP:(i + 1) * SUP] = value
                else:
                    part[off, self.rows(), i * SUP:(i + 1) * SUP] = value.astype(BF16)

        def far(self):
            self.term(2)
            for sign, dev, rows, _, _ in self.ways:
                self.opp[sign] = self.links.start(part.at[2, rows], rs_in.at[0, rows], devs[dev], rs_in.at[0, rows])

        def near(self):
            self.term(1)
            self.term(3)
            for sign, dev, _, others, slot in self.ways:
                land = rs_in.at[1 if sign == 1 else 2, others]
                self.tail.append(self.links.start(part.at[slot, others], land, devs[dev], land))

        def relay(self):
            for sign, dev, rows, _, slot in self.ways:
                self.opp[sign].wait_recv()
                part[slot, rows, :] = (part[slot, rows, :].astype(F32) + rs_in[0, rows, :].astype(F32)).astype(BF16)
                land = rs_in.at[1 if sign == 1 else 2, rows]
                self.tail.append(self.links.start(part.at[slot, rows], land, devs[dev], land))

        def wait(self):
            for incoming in self.tail:
                incoming.wait_recv()

        def total(self, i):
            rows = pl.ds(pl.multiple_of(self.base + i * 16, 16), 16)
            return own_part[rows, :] + rs_in[1, rows, :].astype(F32) + rs_in[2, rows, :].astype(F32)

    def finish(summed, extra):
        def body(i, _):
            rows = pl.ds(pl.multiple_of(i * 16, 16), 16)
            branch = summed.total(i)
            if extra is not None:
                branch += extra[rows, :].astype(F32)
            updated = xbuf[0, x, rows, :].astype(F32) + modv[0, 2, 0:1, lanes_own] * branch
            pos = lax.broadcasted_iota(jnp.int32, (16, 1), 0) + i * 16
            res[rows, :] = jnp.where(pos < e3, updated, 0.0).astype(BF16)
            return 0

        lax.fori_loop(0, SLOT // 16, body, 0)

    def share_x(links, r, inc):
        def own():
            for sign, dev in ((1, "x+"), (-1, "x-")):
                inc["x", r, sign] = links.start(xbuf.at[r, x], xbuf.at[r, xi(-sign)], devs[dev])

        def relay(sign):
            rows = pl.ds(0 if sign == 1 else half_rows, half_rows)
            inc["x", r, sign].wait_recv()
            inc["xh", r, sign] = links.start(
                xbuf.at[r, xi(-sign), rows], xbuf.at[r, xi(-2 * sign), rows], devs["x+" if sign == 1 else "x-"]
            )

        def fin():
            for sign in (1, -1):
                inc["xh", r, sign].wait_recv()

        return own, relay, fin

    def open_gate():
        pl.semaphore_signal(gate_sem, inc=1, device_id=devs["mate"], device_id_type=MESH)

    @pl.when(s == 0)
    def _():
        links = Links(send_sem, recv_sem)
        mate_y = NY - 1 - y
        near_y = y + 1 - 2 * lax.rem(y, 2)
        ways = dict(devs)
        ways["pair"] = (s, z * NY + mate_y, x)
        ways["near"] = (s, z * NY + near_y, x)
        low = pl.ds(0, half_lanes)
        qkv = PairGather(links, (y, z), ways, (
            [qkv_hbm.at[:, :, other]],
            lambda yy: [wbuf.at[:, z, yy, :, low]],
            lambda zz, yy: wbuf.at[0, zz, yy, :, low],
            lambda zz, h: wbuf.at[0, zz, pl.ds(2 * h, 2), :, low],
            lambda zz, yy: wbuf.at[pl.ds(1, 2), zz, yy, :, low],
        ))
        a_low, b_low = pl.ds(0, OA2), pl.ds(0, OB2)
        out = PairGather(links, (y, z), ways, (
            [out_hbm.at[:, out_lanes(1 - group, OA2, 0)], out_hbm.at[:, out_lanes(1 - group, OB2, OA2)]],
            lambda yy: [woa.at[z, yy, :, a_low], wob.at[z, yy, :, b_low]],
            lambda zz, yy: woa.at[zz, yy, :, a_low],
            lambda zz, h: woa.at[zz, pl.ds(2 * h, 2), :, a_low],
            lambda zz, yy: wob.at[zz, yy, :, b_low],
        ))
        inc = {}
        shares = [share_x(links, r, inc) for r in range(2)]

        def send_small():
            inc["f"] = links.start(feats_ref, feats_in, ways["pair"], feats_in)
            inc["m"] = links.start(marks_ref, marks.at[1], ways["pair"], marks.at[1])

        def send_hidden():
            inc["xc"] = links.start(hidden_hbm, xbuf.at[1, x], ways["pair"], xbuf.at[1, x])

        def send_stale():
            inc["sk"] = links.start(keys_hbm.at[:, other], stk2.at[1], ways["pair"], stk2.at[1])
            inc["sv"] = links.start(values_hbm.at[:, other], stv2.at[1], ways["pair"], stv2.at[1])

        def x_own(r):
            if r == 0:
                load_x.wait()
            else:
                inc["xc"].wait_recv()
            shares[r][0]()

        def x_relay(r, sign):
            shares[r][1](sign)

        def modulations():
            load_mod.wait()
            modulation(0, feats_ref)
            inc["f"].wait_recv()
            modulation(1, feats_in)

        def project(offs, first):
            def body(t, _):
                j = t // 2
                rows = pl.ds(pl.multiple_of(lax.rem(t, 2) * SLOT, SLOT), SLOT)
                total = None
                for off in offs:
                    zz = qkv.zi(off)
                    block = wbuf[j, zz, :, :, low].reshape(SUP, half_lanes)
                    term = jnp.dot(xm[zz, rows, :], block, preferred_element_type=F32)
                    total = term if total is None else total + term
                if first:
                    acc2[j, rows, :] = total
                else:
                    acc2[j, rows, :] += total
                return 0

            lax.fori_loop(0, 6, body, 0)

        def attend(first_item, items):
            def body(t, _):
                r = t // 3
                rows = pl.ds(pl.multiple_of(r * SLOT, SLOT), SLOT)
                lanes = pl.ds(pl.multiple_of(lax.rem(t, 3) * HD, HD), HD)
                att2[rows, lanes] = attend_head(
                    acc2[0, rows, lanes], acc2[1, rows, lanes], acc2[2, rows, lanes],
                    stk2[r, :, lanes], stv2[r, :, lanes], marks[r],
                )
                return 0

            lax.fori_loop(first_item, first_item + items, body, 0)

        def block_of(base):
            rows = pl.ds(base, SLOT)

            def block(zz):
                value = nt_dot(att2[rows, 0:OA2], woa[zz, :, :, a_low].reshape(SUP, OA2))
                return value + nt_dot(att2[rows, OA2:OA2 + OB2], wob[zz, :, :, b_low].reshape(SUP, OB2))

            return block

        def reduce_and_finish():
            theirs, ours = Summed(links, SLOT, block_of(SLOT)), Summed(links, 0, block_of(0))
            theirs.far()
            theirs.near()
            ours.far()
            theirs.relay()
            ours.near()
            theirs.term(0)
            theirs.wait()

            def body(i, _):
                att_rows = pl.ds(pl.multiple_of(i * 16, 16), 16)
                part[0, att_rows, :] = theirs.total(i).astype(BF16)
                return 0

            lax.fori_loop(0, SLOT // 16, body, 0)
            paired = links.start(part.at[0, pl.ds(0, SLOT)], pair_in, ways["pair"], pair_in)
            ours.relay()
            ours.term(0)
            ours.wait()
            paired.wait_recv()
            finish(ours, pair_in)

        halves[0].wait()
        send_small()
        qkv.inject()
        send_hidden()
        out.inject()
        send_stale()
        qkv.ya_own(0)
        qkv.zb_own(0, 1)
        qkv.zb_own(0, -1)
        halves[1].wait()
        halves[2].wait()
        out.ya_own(0)
        qkv.yb_own(0, 0)
        out.zb_own(0, 1)
        out.zb_own(0, -1)
        out.yb_own(0, 0)
        x_own(0)
        modulations()
        qkv.zb_relay(0, 1, 1)
        qkv.zb_relay(0, -1, 1)
        qkv.yb_own(-1, 0)
        qkv.yb_own(1, 0)
        out.zb_relay(0, 1, 1)
        out.zb_relay(0, -1, 1)
        out.yb_own(-1, 0)
        out.yb_own(1, 0)
        qkv.ya_own(1)
        qkv.zb_own(1, 1)
        qkv.zb_own(1, -1)
        qkv.yb_own(0, 1)
        x_relay(0, 1)
        x_relay(0, -1)
        qkv.zb_relay(0, 1, 2)
        qkv.zb_relay(0, -1, 2)
        qkv.yb_own(-2, 0)
        out.zb_relay(0, 1, 2)
        out.zb_relay(0, -1, 2)
        qkv.yb_own(2, 0)
        x_own(1)
        qkv.zb_relay(1, 1, 1)
        qkv.zb_relay(1, -1, 1)
        qkv.yb_own(-1, 1)
        out.zb_own(1, 1)
        out.zb_own(1, -1)
        qkv.za_own(0)
        qkv.za_own(1)
        shares[0][2]()
        layer_norm(0, 1)
        qkv.zb_relay(0, 1, 3)
        layer_norm(1, 1)
        out.ya_own(1)
        qkv.yb_own(-3, 0)
        layer_norm(2, 1)
        out.zb_relay(0, 1, 3)
        layer_norm(3, 1)
        qkv.zb_relay(1, 1, 2)
        qkv.zb_relay(1, -1, 2)
        out.zb_relay(1, -1, 1)
        qkv.yb_own(3, 0)
        out.zb_relay(1, 1, 1)
        qkv.za_relay(1, 1, 0)
        qkv.za_relay(-1, 1, 0)
        qkv.yb_own(1, 1)
        x_relay(1, 1)
        x_relay(1, -1)
        qkv.za_relay(1, 1, 1)
        qkv.za_relay(-1, 1, 1)
        qkv.yb_own(-2, 1)
        out.za_own(0)
        qkv.zb_relay(1, -1, 3)
        qkv.yb_own(4, 0)
        out.zb_relay(1, -1, 2)
        out.za_own(1)
        shares[1][2]()
        layer_norm(4, 1)
        layer_norm(5, 1)
        qkv.yb_own(2, 1)
        qkv.za_relay(-1, 2, 0)
        out.zb_relay(1, 1, 2)
        layer_norm(6, 1)
        layer_norm(7, 1)
        qkv.fin(0)
        project((0,), True)
        qkv.yb_own(-3, 1)
        qkv.za_relay(1, 2, 0)
        qkv.za_relay(-1, 2, 1)
        qkv.fin(-1)
        project((-1,), False)
        qkv.yb_own(3, 1)
        qkv.za_relay(1, 2, 1)
        out.za_relay(-1, 1, 0)
        qkv.fin(1)
        project((1,), False)
        qkv.fin(-2)
        project((-2,), False)
        qkv.yb_own(4, 1)
        out.zb_relay(1, -1, 3)
        out.za_relay(1, 1, 0)
        out.za_relay(1, 1, 1)
        out.za_relay(-1, 1, 1)
        out.yb_own(-2, 0)
        out.yb_own(2, 0)
        out.yb_own(-3, 0)
        qkv.fin(2)
        project((2,), False)
        qkv.za_relay(1, 3, 0)
        out.yb_own(3, 0)
        out.yb_own(4, 0)
        out.yb_own(0, 1)
        out.yb_own(-1, 1)
        out.yb_own(1, 1)
        qkv.za_relay(-1, 3, 1)
        out.yb_own(-2, 1)
        qkv.fin(-3)
        project((-3,), False)
        out.yb_own(2, 1)
        out.yb_own(-3, 1)
        out.yb_own(3, 1)
        out.za_relay(-1, 2, 0)
        out.za_relay(1, 2, 0)
        out.yb_own(4, 1)
        qkv.fin(3)
        project((3,), False)
        out.za_relay(1, 2, 1)
        out.za_relay(-1, 2, 1)
        open_gate()
        qkv.fin(4)
        project((4,), False)
        halves[3].wait()
        halves[4].wait()
        inc["sk"].wait_recv()
        inc["sv"].wait_recv()
        inc["m"].wait_recv()
        attend(0, 1)
        out.za_relay(1, 3, 0)
        attend(1, 1)
        out.za_relay(-1, 3, 1)
        attend(2, 1)
        attend(3, 1)
        attend(4, 1)
        attend(5, 1)
        out.fin(0)
        out.fin(-1)
        out.fin(1)
        out.fin(-2)
        out.fin(2)
        out.fin(-3)
        out.fin(3)
        out.fin(4)
        reduce_and_finish()
        handed.start()
        result_ref[...] = res[...]
        handed.wait_send()
        for copy in links.started:
            copy.wait_send()

    @pl.when(s == 1)
    def _():
        links = Links(send_sem, recv_sem)
        qkv = Gather(links, (y, z), devs, (
            lambda zz, yy: wbuf.at[0, zz, yy],
            lambda zz, yy, h: wbuf.at[0, zz, yy, pl.ds(h * (KB // 2), KB // 2)],
            lambda zz, h: wbuf.at[0, zz, pl.ds(2 * h, 2)],
            lambda zz, yy: wbuf.at[pl.ds(1, 2), zz, yy],
            lambda zz, yy, h: wbuf.at[1 + h, zz, yy],
        ))
        out = Gather(links, (y, z), devs, (
            lambda zz, yy: woa.at[zz, yy],
            lambda zz, yy, h: woa.at[zz, yy, pl.ds(h * (KB // 2), KB // 2)],
            lambda zz, h: woa.at[zz, pl.ds(2 * h, 2)],
            lambda zz, yy: wob.at[zz, yy],
            lambda zz, yy, h: wob.at[zz, yy, pl.ds(h * (KB // 2), KB // 2)],
        ))
        inc = {}
        share = share_x(links, 0, inc)

        def x_start():
            handed.wait_recv()
            share[0]()

        def x_relay(sign):
            share[1](sign)

        def x_fin():
            share[2]()

        def modulations():
            load_mod.wait()
            modulation(0, feats_ref)

        rows = pl.ds(0, SLOT)

        def project(offs, first):
            def body(t, _):
                j = t // 3
                lanes = pl.ds(pl.multiple_of(lax.rem(t, 3) * 256, 256), 256)
                total = None
                for off in offs:
                    zz = qkv.zi(off)
                    block = wbuf[j, zz, :, :, lanes].reshape(SUP, 256)
                    term = jnp.dot(xm[zz, rows, :], block, preferred_element_type=F32)
                    total = term if total is None else total + term
                if first:
                    acc[j, :, lanes] = total
                else:
                    acc[j, :, lanes] += total
                return 0

            lax.fori_loop(0, 9, body, 0)

        def attend(first_head, heads):
            def body(h, _):
                lanes = pl.ds(pl.multiple_of(h * HD, HD), HD)
                att[:, lanes] = attend_head(
                    acc[0, :, lanes], acc[1, :, lanes], acc[2, :, lanes], stk[:, lanes], stv[:, lanes], marks[0]
                )
                return 0

            lax.fori_loop(first_head, first_head + heads, body, 0)

        def block(zz):
            value = nt_dot(att[:, 0:OA], woa[zz].reshape(SUP, OA))
            return value + nt_dot(att[:, OA:CW], wob[zz].reshape(SUP, OB))

        def reduce_and_finish():
            ours = Summed(links, 0, block)
            ours.far()
            ours.near()
            ours.relay()
            ours.term(0)
            ours.wait()
            finish(ours, None)

        whole[0].wait()
        pl.semaphore_wait(gate_sem, 1)
        qkv.ya_own()
        qkv.zb_own(1)
        qkv.zb_own(-1)
        whole[1].wait()
        whole[2].wait()
        out.ya_own()
        qkv.yb_own(0)
        out.zb_own(1)
        out.zb_own(-1)
        modulations()
        out.yb_own(0)
        qkv.ya_relay(1)
        qkv.ya_relay(-1)
        out.ya_relay(1)
        out.ya_relay(-1)
        qkv.zb_relay(1, 1)
        qkv.zb_relay(-1, 1)
        qkv.yb_own(-1)
        out.zb_relay(1, 1)
        out.zb_relay(-1, 1)
        qkv.yb_own(1)
        qkv.za_own(0)
        qkv.za_own(1)
        qkv.yb_relay(0, 1)
        qkv.yb_relay(0, -1)
        qkv.zb_relay(1, 2)
        qkv.zb_relay(-1, 2)
        qkv.yb_own(-2)
        qkv.za_relay(1, 1, 0)
        qkv.za_relay(-1, 1, 0)
        qkv.yb_relay(-1, 1)
        qkv.yb_relay(-1, -1)
        qkv.yb_relay(1, 1)
        qkv.yb_relay(1, -1)
        qkv.za_relay(1, 1, 1)
        qkv.za_relay(-1, 1, 1)
        qkv.yb_own(2)
        qkv.zb_relay(1, 3)
        qkv.zb_relay(-1, 3)
        qkv.yb_relay(-2, 1)
        qkv.yb_relay(-2, -1)
        out.za_own(0)
        qkv.yb_own(-3)
        qkv.za_relay(1, 2, 0)
        qkv.za_relay(-1, 2, 0)
        qkv.yb_own(3)
        qkv.za_relay(1, 2, 1)
        qkv.za_relay(-1, 2, 1)
        qkv.yb_relay(2, 1)
        qkv.yb_relay(2, -1)
        qkv.yb_own(4)
        out.za_own(1)
        x_start()
        out.zb_relay(1, 2)
        out.zb_relay(-1, 2)
        qkv.za_relay(1, 3, 0)
        out.za_relay(-1, 1, 0)
        qkv.yb_relay(-3, 1)
        qkv.yb_relay(-3, -1)
        qkv.yb_relay(3, 1)
        qkv.yb_relay(3, -1)
        qkv.za_relay(-1, 3, 1)
        out.za_relay(1, 1, 0)
        x_relay(1)
        x_relay(-1)
        out.yb_relay(0, 1)
        out.yb_relay(0, -1)
        out.yb_own(-1)
        out.yb_own(1)
        out.yb_own(-2)
        out.za_relay(1, 1, 1)
        out.zb_relay(-1, 3)
        out.yb_own(2)
        out.za_relay(-1, 1, 1)
        qkv.yb_relay(4, 1)
        qkv.yb_relay(4, -1)
        x_fin()
        layer_norm(0, 1)
        out.zb_relay(1, 3)
        out.yb_own(-3)
        out.za_relay(-1, 2, 0)
        layer_norm(1, 1)
        out.yb_own(3)
        layer_norm(2, 1)
        layer_norm(3, 1)
        qkv.fin(0)
        qkv.fin(-1)
        qkv.fin(1)
        project((0, -1, 1), True)
        out.yb_relay(-1, 1)
        out.yb_relay(-1, -1)
        out.yb_relay(1, 1)
        out.yb_relay(1, -1)
        out.yb_relay(-2, 1)
        out.yb_relay(-2, -1)
        out.yb_relay(2, 1)
        out.yb_relay(2, -1)
        out.za_relay(1, 2, 0)
        qkv.fin(-2)
        qkv.fin(2)
        project((-2, 2), False)
        out.yb_relay(-3, 1)
        out.yb_relay(-3, -1)
        out.yb_own(4)
        out.yb_relay(3, 1)
        out.yb_relay(3, -1)
        out.za_relay(1, 2, 1)
        out.za_relay(-1, 2, 1)
        qkv.fin(-3)
        qkv.fin(3)
        project((-3, 3), False)
        qkv.fin(4)
        project((4,), False)
        out.yb_relay(4, 1)
        out.yb_relay(4, -1)
        out.za_relay(1, 3, 0)
        whole[3].wait()
        whole[4].wait()
        attend(0, 1)
        attend(1, 1)
        out.za_relay(-1, 3, 1)
        attend(2, 1)
        attend(3, 1)
        attend(4, 1)
        attend(5, 1)
        out.fin(0)
        out.fin(-1)
        out.fin(1)
        out.fin(-2)
        out.fin(2)
        out.fin(-3)
        out.fin(3)
        out.fin(4)
        reduce_and_finish()
        result_ref[...] = res[...]
        for copy in links.started:
            copy.wait_send()


def shards(
    hidden_in, patch_ends, timestep, mod_weight, qkv_weight, out_weight, stale_keys, stale_values
):
    feats = jnp.broadcast_to(embed_time(timestep), (16, FREQ))
    marks = jnp.broadcast_to(jnp.pad(patch_ends, ((0, 0), (0, HD - patch_ends.shape[1]))), (8, HD))
    mod_mat = jnp.swapaxes(mod_weight[0], 0, 1)
    qkv_mat = jnp.swapaxes(qkv_weight[0], 0, 1)
    out_mat = jnp.swapaxes(out_weight[0], 0, 1)
    anywhere = pl.BlockSpec(memory_space=pl.ANY)
    vmem = pl.BlockSpec(memory_space=pltpu.VMEM)
    half = CW // 2
    result = pl.pallas_call(
        kernel,
        out_shape=jax.ShapeDtypeStruct((SLOT, CW), BF16),
        in_specs=[pl.BlockSpec(memory_space=pltpu.SMEM), vmem, vmem] + [anywhere] * 6,
        out_specs=vmem,
        scratch_shapes=[
            pltpu.VMEM((3, NZ, NY, KB, CW), BF16),
            pltpu.VMEM((NZ, NY, KB, OA), BF16),
            pltpu.VMEM((NZ, NY, KB, OB), BF16),
            pltpu.VMEM((3, FREQ, NX * CW), BF16),
            pltpu.VMEM((2, 3, 16, NX * CW), F32),
            pltpu.VMEM((2, NX, SLOT, CW), BF16),
            pltpu.VMEM((NZ, 2 * SLOT, SUP), BF16),
            pltpu.VMEM((3, SLOT, CW), F32),
            pltpu.VMEM((3, 2 * SLOT, half), F32),
            pltpu.VMEM((SLOT, CW), BF16),
            pltpu.VMEM((SLOT, CW), BF16),
            pltpu.VMEM((2, SLOT, half), BF16),
            pltpu.VMEM((2, SLOT, half), BF16),
            pltpu.VMEM((SLOT, CW), BF16),
            pltpu.VMEM((2 * SLOT, half), BF16),
            pltpu.VMEM((NX, 2 * SLOT, CW), BF16),
            pltpu.VMEM((2 * SLOT, CW), F32),
            pltpu.VMEM((3, 2 * SLOT, CW), BF16),
            pltpu.VMEM((SLOT, CW), BF16),
            pltpu.VMEM((16, FREQ), BF16),
            pltpu.VMEM((2, 8, HD), jnp.int32),
            pltpu.VMEM((SLOT, CW), BF16),
            pltpu.SemaphoreType.DMA((N_SEM,)),
            pltpu.SemaphoreType.DMA((N_SEM,)),
            pltpu.SemaphoreType.DMA((8,)),
            pltpu.SemaphoreType.DMA((2,)),
            pltpu.SemaphoreType.REGULAR,
        ],
        compiler_params=pltpu.CompilerParams(
            collective_id=0, has_side_effects=True, vmem_limit_bytes=62 * 1024 * 1024
        ),
        name="patch_layers",
    )(
        patch_ends, feats, marks, hidden_in[0], mod_mat, qkv_mat, out_mat,
        stale_keys[0, 0], stale_values[0, 0],
    )
    return result[None, None]


def solution(mesh):
    return jax.shard_map(
        shards,
        mesh=mesh,
        in_specs=(
            P("row", None, "col"),
            P("row", None),
            P("row"),
            P("section", None, None, None),
            P("section", "row", None, "col"),
            P("section", "col", "row"),
            P("section", "row", None, "col"),
            P("section", "row", None, "col"),
        ),
        out_specs=P("section", "row", None, "col"),
        check_vma=False,
    )
```

time: 544 us -> 130 us (0.24)
  waiting for transfers between devices: 250 us -> 0 us
  Pallas kernels: 0 us -> 125 us
  blocking collectives: 91 us -> 0 us
  matrix products: 76.4 us -> 0 us
  local copies, waits for them, and re-layouts: 61.6 us -> 3.62 us
  other arithmetic: 34.5 us -> 0.06 us
  between operations: 21.4 us -> 0.67 us
  starting transfers between devices: 5.63 us -> 0 us
    all_gather x2 -> x0, waiting for transfers between devices: 130 us -> none  [the longest x1 85.1 us: shards(): qkv_full = lax.all_gather(qkv_weight, 'row', axis=1, tiled=True)]
    pallas_call x0 -> x1, Pallas kernels: none -> 125 us  [shards(): pl.pallas_call(kernel, out_shape=jax.ShapeDtypeStruct((SLOT, CW), BF16),...]
    reduce_scatter x5 -> x0, waiting for transfers between devices: 106 us -> none  [shards(): lax.psum_scatter(partial_out.astype(jnp.bfloat16), 'col', scatter_dimensi...]
    dot_general x21 -> x0, matrix products: 76.4 us -> none  [the longest x5 47.1 us: shards(): jnp.dot(modulated.reshape(-1, feat_width), qkv_matrix, preferred_element_...]
    all_gather x5 -> x0, blocking collectives: 55 us -> none  [modulated_rows(): return lax.all_gather(local_rows, 'col', axis=2, tiled=True)]
    psum x5 -> x0, blocking collectives: 36.1 us -> none  [modulated_rows(): lax.psum((jnp.sum(as_float, axis=-1), jnp.sum(as_float * as_float, axis=-...]
    another operation x13 -> x1, other arithmetic: 27.2 us -> 0.05 us
    scatter x15 -> x0, local copies, waits for them, and re-layouts: 22.2 us -> none  [update_one(): return lax.dynamic_update_slice_in_dim(source, new_rows, first_row, 0)]
  transfers between devices with their start and end apart: 11 -> 0, of which waited for: 11 -> 0; matrix products, arithmetic and copies ran while one was open for 13% -> 0% of each run, Pallas kernels for 0% -> 0%
where the time goes in v3:
time: 130 us
  Pallas kernels  125 us (96%)
  local copies, waits for them, and re-layouts  3.62 us (3%)
    pallas_call x1, Pallas kernels, shards(): pl.pallas_call(kernel, out_shape=jax.ShapeDtypeStruct((SLOT, CW), BF16),...  125 us

profile of v3, /device:TPU:1, one launch (start us, length us, event | category | flops | bytes accessed | tf_op | source)
XLA Modules:
  0.0 129.7 jit_solution(6262819265587544663)
XLA Ops:
  0.7 0.7 pad_bitcast_fusion
  1.4 0.6 broadcast_in_dim.19.marks_ref
  2.0 0.6 broadcast_in_dim.8.feats_ref
  2.6 125.3 %patch_layers.1 = bf16[256,768]{1,0:T(8,128)(2,1)} custom-call(s32[1,4]{1,0:T(1,128)} %ends_ref.1, bf16[16,256]{1,0:T(8,128)(2,1)} %broadcast_in_dim.8.feats_ref, s32[8,128]{1,0:T(8,128)} %broadcast_in_dim.19.marks_ref, bf16[256,768]{1,0:T(8,128)(2,1)} %bitcast.19, bf16[3,256,3072]{2,1,0:T(8,128)(2,1)} %bitcast.16, bf16[3,96,768]{2,1,0:T(8,128)(2,1)} %bitcast.18, ...), custom_call_target="tpu_custom_call" | custom-call | tf_op jit(solution)/shard_map/patch_layers/pallas_call | solution.py:940
  127.9 1.8 %copy.11 = bf16[1,1,256,768]{3,2,1,0:T(8,128)(2,1)} copy(bf16[1,1,256,768]{3,2,1,0:T(8,128)(2,1)} %bitcast.17) | data formatting | bytes 786432
  (2 shorter events, 0.1 us)

commit v4 on v3

--- a/solution.py
+++ b/solution.py
@@ -226,6 +226,16 @@
 
 def nt_dot(left, right):
     return lax.dot_general(left, right, (((1,), (1,)), ((), ())), preferred_element_type=F32)
+
+
+def pairs_dot(lefts, rights):
+    total = None
+    for i in range(0, len(lefts), 2):
+        left = jnp.concatenate(lefts[i:i + 2], axis=1)
+        right = jnp.concatenate(rights[i:i + 2], axis=0)
+        term = jnp.dot(left, right, preferred_element_type=F32)
+        total = term if total is None else total + term
+    return total
 
 
 def kernel(
@@ -493,12 +503,10 @@
             def body(t, _):
                 j = t // 2
                 rows = pl.ds(pl.multiple_of(lax.rem(t, 2) * SLOT, SLOT), SLOT)
-                total = None
-                for off in offs:
-                    zz = qkv.zi(off)
-                    block = wbuf[j, zz, :, :, low].reshape(SUP, half_lanes)
-                    term = jnp.dot(xm[zz, rows, :], block, preferred_element_type=F32)
-                    total = term if total is None else total + term
+                total = pairs_dot(
+                    [xm[qkv.zi(off), rows, :] for off in offs],
+                    [wbuf[j, qkv.zi(off), :, :, low].reshape(SUP, half_lanes) for off in offs],
+                )
                 if first:
                     acc2[j, rows, :] = total
                 else:
@@ -533,8 +541,8 @@
             theirs, ours = Summed(links, SLOT, block_of(SLOT)), Summed(links, 0, block_of(0))
             theirs.far()
             theirs.near()
+            theirs.relay()
             ours.far()
-            theirs.relay()
             ours.near()
             theirs.term(0)
             theirs.wait()
@@ -634,19 +642,17 @@
         layer_norm(6, 1)
         layer_norm(7, 1)
         qkv.fin(0)
-        project((0,), True)
+        qkv.fin(-1)
+        project((0, -1), True)
         qkv.yb_own(-3, 1)
         qkv.za_relay(1, 2, 0)
         qkv.za_relay(-1, 2, 1)
-        qkv.fin(-1)
-        project((-1,), False)
-        qkv.yb_own(3, 1)
         qkv.za_relay(1, 2, 1)
         out.za_relay(-1, 1, 0)
+        qkv.yb_own(3, 1)
         qkv.fin(1)
-        project((1,), False)
         qkv.fin(-2)
-        project((-2,), False)
+        project((1, -2), False)
         qkv.yb_own(4, 1)
         out.zb_relay(1, -1, 3)
         out.za_relay(1, 1, 0)
@@ -655,8 +661,6 @@
         out.yb_own(-2, 0)
         out.yb_own(2, 0)
         out.yb_own(-3, 0)
-        qkv.fin(2)
-        project((2,), False)
         qkv.za_relay(1, 3, 0)
         out.yb_own(3, 0)
         out.yb_own(4, 0)
@@ -665,28 +669,28 @@
         out.yb_own(1, 1)
         qkv.za_relay(-1, 3, 1)
         out.yb_own(-2, 1)
+        qkv.fin(2)
         qkv.fin(-3)
-        project((-3,), False)
+        project((2, -3), False)
         out.yb_own(2, 1)
         out.yb_own(-3, 1)
         out.yb_own(3, 1)
+        out.yb_own(4, 1)
         out.za_relay(-1, 2, 0)
         out.za_relay(1, 2, 0)
-        out.yb_own(4, 1)
-        qkv.fin(3)
-        project((3,), False)
         out.za_relay(1, 2, 1)
         out.za_relay(-1, 2, 1)
         open_gate()
+        qkv.fin(3)
         qkv.fin(4)
-        project((4,), False)
+        project((3, 4), False)
+        out.za_relay(1, 3, 0)
         halves[3].wait()
         halves[4].wait()
         inc["sk"].wait_recv()
         inc["sv"].wait_recv()
         inc["m"].wait_recv()
         attend(0, 1)
-        out.za_relay(1, 3, 0)
         attend(1, 1)
         out.za_relay(-1, 3, 1)
         attend(2, 1)
@@ -748,12 +752,10 @@
             def body(t, _):
                 j = t // 3
                 lanes = pl.ds(pl.multiple_of(lax.rem(t, 3) * 256, 256), 256)
-                total = None
-                for off in offs:
-                    zz = qkv.zi(off)
-                    block = wbuf[j, zz, :, :, lanes].reshape(SUP, 256)
-                    term = jnp.dot(xm[zz, rows, :], block, preferred_element_type=F32)
-                    total = term if total is None else total + term
+                total = pairs_dot(
+                    [xm[qkv.zi(off), rows, :] for off in offs],
+                    [wbuf[j, qkv.zi(off), :, :, lanes].reshape(SUP, 256) for off in offs],
+                )
                 if first:
                     acc[j, :, lanes] = total
                 else:
@@ -796,8 +798,8 @@
         qkv.yb_own(0)
         out.zb_own(1)
         out.zb_own(-1)
+        out.yb_own(0)
         modulations()
-        out.yb_own(0)
         qkv.ya_relay(1)
         qkv.ya_relay(-1)
         out.ya_relay(1)
@@ -805,109 +807,108 @@
         qkv.zb_relay(1, 1)
         qkv.zb_relay(-1, 1)
         qkv.yb_own(-1)
+        qkv.yb_own(1)
         out.zb_relay(1, 1)
         out.zb_relay(-1, 1)
-        qkv.yb_own(1)
+        out.yb_own(-1)
+        out.yb_own(1)
+        qkv.yb_relay(0, 1)
+        qkv.yb_relay(0, -1)
         qkv.za_own(0)
         qkv.za_own(1)
-        qkv.yb_relay(0, 1)
-        qkv.yb_relay(0, -1)
+        out.za_own(0)
+        out.yb_relay(0, 1)
+        out.yb_relay(0, -1)
         qkv.zb_relay(1, 2)
         qkv.zb_relay(-1, 2)
         qkv.yb_own(-2)
+        qkv.yb_relay(-1, 1)
+        qkv.yb_relay(-1, -1)
+        out.za_own(1)
+        qkv.yb_own(2)
         qkv.za_relay(1, 1, 0)
         qkv.za_relay(-1, 1, 0)
-        qkv.yb_relay(-1, 1)
-        qkv.yb_relay(-1, -1)
         qkv.yb_relay(1, 1)
         qkv.yb_relay(1, -1)
         qkv.za_relay(1, 1, 1)
         qkv.za_relay(-1, 1, 1)
-        qkv.yb_own(2)
-        qkv.zb_relay(1, 3)
-        qkv.zb_relay(-1, 3)
-        qkv.yb_relay(-2, 1)
-        qkv.yb_relay(-2, -1)
-        out.za_own(0)
-        qkv.yb_own(-3)
-        qkv.za_relay(1, 2, 0)
-        qkv.za_relay(-1, 2, 0)
-        qkv.yb_own(3)
-        qkv.za_relay(1, 2, 1)
-        qkv.za_relay(-1, 2, 1)
-        qkv.yb_relay(2, 1)
-        qkv.yb_relay(2, -1)
-        qkv.yb_own(4)
-        out.za_own(1)
-        x_start()
-        out.zb_relay(1, 2)
-        out.zb_relay(-1, 2)
-        qkv.za_relay(1, 3, 0)
-        out.za_relay(-1, 1, 0)
-        qkv.yb_relay(-3, 1)
-        qkv.yb_relay(-3, -1)
-        qkv.yb_relay(3, 1)
-        qkv.yb_relay(3, -1)
-        qkv.za_relay(-1, 3, 1)
-        out.za_relay(1, 1, 0)
-        x_relay(1)
-        x_relay(-1)
-        out.yb_relay(0, 1)
-        out.yb_relay(0, -1)
-        out.yb_own(-1)
-        out.yb_own(1)
-        out.yb_own(-2)
-        out.za_relay(1, 1, 1)
-        out.zb_relay(-1, 3)
-        out.yb_own(2)
-        out.za_relay(-1, 1, 1)
-        qkv.yb_relay(4, 1)
-        qkv.yb_relay(4, -1)
-        x_fin()
-        layer_norm(0, 1)
-        out.zb_relay(1, 3)
-        out.yb_own(-3)
-        out.za_relay(-1, 2, 0)
-        layer_norm(1, 1)
-        out.yb_own(3)
-        layer_norm(2, 1)
-        layer_norm(3, 1)
-        qkv.fin(0)
-        qkv.fin(-1)
-        qkv.fin(1)
-        project((0, -1, 1), True)
         out.yb_relay(-1, 1)
         out.yb_relay(-1, -1)
         out.yb_relay(1, 1)
         out.yb_relay(1, -1)
+        out.zb_relay(1, 2)
+        out.zb_relay(-1, 2)
+        out.yb_own(-2)
+        out.yb_own(2)
+        qkv.yb_relay(-2, 1)
+        qkv.yb_relay(-2, -1)
+        qkv.zb_relay(1, 3)
+        qkv.zb_relay(-1, 3)
+        qkv.yb_own(-3)
+        out.za_relay(1, 1, 0)
+        out.za_relay(-1, 1, 0)
+        qkv.yb_own(3)
+        out.za_relay(1, 1, 1)
+        out.za_relay(-1, 1, 1)
+        qkv.za_relay(1, 2, 0)
+        qkv.za_relay(-1, 2, 0)
+        qkv.yb_relay(2, 1)
+        qkv.yb_relay(2, -1)
         out.yb_relay(-2, 1)
         out.yb_relay(-2, -1)
         out.yb_relay(2, 1)
         out.yb_relay(2, -1)
+        qkv.za_relay(1, 2, 1)
+        x_start()
+        qkv.za_relay(-1, 2, 1)
+        qkv.yb_own(4)
+        out.zb_relay(1, 3)
+        out.zb_relay(-1, 3)
+        out.yb_own(-3)
+        qkv.yb_relay(-3, 1)
+        qkv.yb_relay(-3, -1)
         out.za_relay(1, 2, 0)
+        out.za_relay(-1, 2, 0)
+        out.yb_own(3)
+        out.za_relay(1, 2, 1)
+        out.za_relay(-1, 2, 1)
+        x_relay(1)
+        x_relay(-1)
+        qkv.yb_relay(3, 1)
+        qkv.yb_relay(3, -1)
+        qkv.za_relay(1, 3, 0)
+        x_fin()
+        layer_norm(0, 1)
+        layer_norm(1, 1)
+        layer_norm(2, 1)
+        layer_norm(3, 1)
+        qkv.yb_relay(4, 1)
+        qkv.yb_relay(4, -1)
+        qkv.za_relay(-1, 3, 1)
+        qkv.fin(0)
+        qkv.fin(-1)
+        qkv.fin(1)
         qkv.fin(-2)
-        qkv.fin(2)
-        project((-2, 2), False)
+        project((0, -1, 1, -2), True)
         out.yb_relay(-3, 1)
         out.yb_relay(-3, -1)
-        out.yb_own(4)
         out.yb_relay(3, 1)
         out.yb_relay(3, -1)
-        out.za_relay(1, 2, 1)
-        out.za_relay(-1, 2, 1)
+        out.yb_own(4)
+        out.za_relay(1, 3, 0)
+        qkv.fin(2)
         qkv.fin(-3)
-        qkv.fin(3)
-        project((-3, 3), False)
-        qkv.fin(4)
-        project((4,), False)
+        project((2, -3), False)
+        out.za_relay(-1, 3, 1)
         out.yb_relay(4, 1)
         out.yb_relay(4, -1)
-        out.za_relay(1, 3, 0)
+        qkv.fin(3)
+        qkv.fin(4)
+        project((3, 4), False)
         whole[3].wait()
         whole[4].wait()
         attend(0, 1)
         attend(1, 1)
-        out.za_relay(-1, 3, 1)
         attend(2, 1)
         attend(3, 1)
         attend(4, 1)

time: 130 us -> 126 us (0.969)
  Pallas kernels: 125 us -> 121 us
    pallas_call x1, Pallas kernels: 125 us -> 121 us  [shards(): pl.pallas_call(kernel, out_shape=jax.ShapeDtypeStruct((SLOT, CW), BF16),...]
where the time goes in v4:
time: 126 us
  Pallas kernels  121 us (96%)
  local copies, waits for them, and re-layouts  3.62 us (3%)
    pallas_call x1, Pallas kernels, shards(): pl.pallas_call(kernel, out_shape=jax.ShapeDtypeStruct((SLOT, CW), BF16),...  121 us

profile of v4, /device:TPU:1, one launch (start us, length us, event | category | flops | bytes accessed | tf_op | source)
XLA Modules:
  0.0 125.6 jit_solution(9085165000600516620)
XLA Ops:
  0.7 0.7 pad_bitcast_fusion
  1.4 0.6 broadcast_in_dim.19.marks_ref
  2.0 0.6 broadcast_in_dim.8.feats_ref
  2.6 121.2 %patch_layers.1 = bf16[256,768]{1,0:T(8,128)(2,1)} custom-call(s32[1,4]{1,0:T(1,128)} %ends_ref.1, bf16[16,256]{1,0:T(8,128)(2,1)} %broadcast_in_dim.8.feats_ref, s32[8,128]{1,0:T(8,128)} %broadcast_in_dim.19.marks_ref, bf16[256,768]{1,0:T(8,128)(2,1)} %bitcast.19, bf16[3,256,3072]{2,1,0:T(8,128)(2,1)} %bitcast.16, bf16[3,96,768]{2,1,0:T(8,128)(2,1)} %bitcast.18, ...), custom_call_target="tpu_custom_call" | custom-call | tf_op jit(solution)/shard_map/patch_layers/pallas_call | solution.py:941
  123.8 1.8 %copy.11 = bf16[1,1,256,768]{3,2,1,0:T(8,128)(2,1)} copy(bf16[1,1,256,768]{3,2,1,0:T(8,128)(2,1)} %bitcast.17) | data formatting | bytes 786432
  (2 shorter events, 0.1 us)

commit v5 on v4

--- a/solution.py
+++ b/solution.py
@@ -22,7 +22,7 @@
 MESH = pl.DeviceIdType.MESH
 F32 = jnp.float32
 BF16 = jnp.bfloat16
-N_SEM = 160
+N_SEM = 176
 
 
 def embed_time(timestep):
@@ -411,7 +411,7 @@
             rows = pl.ds(pl.multiple_of(self.base + i * 16, 16), 16)
             return own_part[rows, :] + rs_in[1, rows, :].astype(F32) + rs_in[2, rows, :].astype(F32)
 
-    def finish(summed, extra):
+    def finish(summed, extra, target):
         def body(i, _):
             rows = pl.ds(pl.multiple_of(i * 16, 16), 16)
             branch = summed.total(i)
@@ -419,25 +419,32 @@
                 branch += extra[rows, :].astype(F32)
             updated = xbuf[0, x, rows, :].astype(F32) + modv[0, 2, 0:1, lanes_own] * branch
             pos = lax.broadcasted_iota(jnp.int32, (16, 1), 0) + i * 16
-            res[rows, :] = jnp.where(pos < e3, updated, 0.0).astype(BF16)
+            target[rows, :] = jnp.where(pos < e3, updated, 0.0).astype(BF16)
             return 0
 
         lax.fori_loop(0, SLOT // 16, body, 0)
 
     def share_x(links, r, inc):
+        rows_of = pl.ds(0, half_rows), pl.ds(half_rows, half_rows)
+        ways = ((1, "x+", 0), (-1, "x-", 1))
+
         def own():
-            for sign, dev in ((1, "x+"), (-1, "x-")):
-                inc["x", r, sign] = links.start(xbuf.at[r, x], xbuf.at[r, xi(-sign)], devs[dev])
+            for step in range(2):
+                for sign, dev, half in ways:
+                    rows = rows_of[half if step == 0 else 1 - half]
+                    inc["x", r, sign, step] = links.start(xbuf.at[r, x, rows], xbuf.at[r, xi(-sign), rows], devs[dev])
 
         def relay(sign):
-            rows = pl.ds(0 if sign == 1 else half_rows, half_rows)
-            inc["x", r, sign].wait_recv()
+            half = 0 if sign == 1 else 1
+            rows = rows_of[half]
+            inc["x", r, sign, 0].wait_recv()
             inc["xh", r, sign] = links.start(
                 xbuf.at[r, xi(-sign), rows], xbuf.at[r, xi(-2 * sign), rows], devs["x+" if sign == 1 else "x-"]
             )
 
         def fin():
             for sign in (1, -1):
+                inc["x", r, sign, 1].wait_recv()
                 inc["xh", r, sign].wait_recv()
 
         return own, relay, fin
@@ -558,7 +565,7 @@
             ours.term(0)
             ours.wait()
             paired.wait_recv()
-            finish(ours, pair_in)
+            finish(ours, pair_in, res)
 
         halves[0].wait()
         send_small()
@@ -586,76 +593,75 @@
         out.zb_relay(0, -1, 1)
         out.yb_own(-1, 0)
         out.yb_own(1, 0)
+        x_relay(0, 1)
+        x_relay(0, -1)
         qkv.ya_own(1)
         qkv.zb_own(1, 1)
         qkv.zb_own(1, -1)
         qkv.yb_own(0, 1)
-        x_relay(0, 1)
-        x_relay(0, -1)
         qkv.zb_relay(0, 1, 2)
         qkv.zb_relay(0, -1, 2)
         qkv.yb_own(-2, 0)
         out.zb_relay(0, 1, 2)
         out.zb_relay(0, -1, 2)
         qkv.yb_own(2, 0)
+        shares[0][2]()
+        layer_norm(0, 1)
         x_own(1)
         qkv.zb_relay(1, 1, 1)
         qkv.zb_relay(1, -1, 1)
+        layer_norm(1, 1)
+        out.ya_own(1)
         qkv.yb_own(-1, 1)
-        out.zb_own(1, 1)
-        out.zb_own(1, -1)
         qkv.za_own(0)
         qkv.za_own(1)
-        shares[0][2]()
-        layer_norm(0, 1)
+        layer_norm(2, 1)
         qkv.zb_relay(0, 1, 3)
-        layer_norm(1, 1)
-        out.ya_own(1)
+        out.zb_own(1, -1)
+        layer_norm(3, 1)
         qkv.yb_own(-3, 0)
-        layer_norm(2, 1)
+        out.zb_own(1, 1)
         out.zb_relay(0, 1, 3)
-        layer_norm(3, 1)
         qkv.zb_relay(1, 1, 2)
         qkv.zb_relay(1, -1, 2)
-        out.zb_relay(1, -1, 1)
+        x_relay(1, 1)
+        x_relay(1, -1)
         qkv.yb_own(3, 0)
-        out.zb_relay(1, 1, 1)
         qkv.za_relay(1, 1, 0)
         qkv.za_relay(-1, 1, 0)
         qkv.yb_own(1, 1)
-        x_relay(1, 1)
-        x_relay(1, -1)
-        qkv.za_relay(1, 1, 1)
+        out.za_own(0)
         qkv.za_relay(-1, 1, 1)
         qkv.yb_own(-2, 1)
-        out.za_own(0)
+        out.zb_relay(1, -1, 1)
+        qkv.za_relay(1, 1, 1)
+        shares[1][2]()
+        layer_norm(4, 1)
         qkv.zb_relay(1, -1, 3)
         qkv.yb_own(4, 0)
-        out.zb_relay(1, -1, 2)
+        layer_norm(5, 1)
         out.za_own(1)
-        shares[1][2]()
-        layer_norm(4, 1)
-        layer_norm(5, 1)
+        layer_norm(6, 1)
+        layer_norm(7, 1)
         qkv.yb_own(2, 1)
         qkv.za_relay(-1, 2, 0)
-        out.zb_relay(1, 1, 2)
-        layer_norm(6, 1)
-        layer_norm(7, 1)
+        out.zb_relay(1, 1, 1)
         qkv.fin(0)
         qkv.fin(-1)
         project((0, -1), True)
         qkv.yb_own(-3, 1)
         qkv.za_relay(1, 2, 0)
+        out.za_relay(-1, 1, 0)
+        out.za_relay(1, 1, 0)
         qkv.za_relay(-1, 2, 1)
+        qkv.yb_own(3, 1)
         qkv.za_relay(1, 2, 1)
-        out.za_relay(-1, 1, 0)
-        qkv.yb_own(3, 1)
+        out.zb_relay(1, -1, 2)
         qkv.fin(1)
         qkv.fin(-2)
         project((1, -2), False)
         qkv.yb_own(4, 1)
-        out.zb_relay(1, -1, 3)
-        out.za_relay(1, 1, 0)
+        out.zb_relay(1, 1, 2)
         out.za_relay(1, 1, 1)
         out.za_relay(-1, 1, 1)
         out.yb_own(-2, 0)
@@ -666,24 +672,25 @@
         out.yb_own(4, 0)
         out.yb_own(0, 1)
         out.yb_own(-1, 1)
+        out.za_relay(-1, 2, 0)
+        out.za_relay(1, 2, 0)
         out.yb_own(1, 1)
+        out.yb_own(-2, 1)
+        out.yb_own(2, 1)
         qkv.za_relay(-1, 3, 1)
-        out.yb_own(-2, 1)
         qkv.fin(2)
         qkv.fin(-3)
         project((2, -3), False)
-        out.yb_own(2, 1)
+        out.zb_relay(1, -1, 3)
+        out.yb_own(3, 1)
         out.yb_own(-3, 1)
-        out.yb_own(3, 1)
-        out.yb_own(4, 1)
-        out.za_relay(-1, 2, 0)
-        out.za_relay(1, 2, 0)
+        out.za_relay(-1, 2, 1)
         out.za_relay(1, 2, 1)
-        out.za_relay(-1, 2, 1)
         open_gate()
         qkv.fin(3)
         qkv.fin(4)
         project((3, 4), False)
+        out.yb_own(4, 1)
         out.za_relay(1, 3, 0)
         halves[3].wait()
         halves[4].wait()
@@ -691,8 +698,8 @@
         inc["sv"].wait_recv()
         inc["m"].wait_recv()
         attend(0, 1)
+        out.za_relay(-1, 3, 1)
         attend(1, 1)
-        out.za_relay(-1, 3, 1)
         attend(2, 1)
         attend(3, 1)
         attend(4, 1)
@@ -785,7 +792,7 @@
             ours.relay()
             ours.term(0)
             ours.wait()
-            finish(ours, None)
+            finish(ours, None, result_ref)
 
         whole[0].wait()
         pl.semaphore_wait(gate_sem, 1)
@@ -869,36 +876,36 @@
         qkv.yb_relay(-3, -1)
         out.za_relay(1, 2, 0)
         out.za_relay(-1, 2, 0)
+        x_relay(1)
+        x_relay(-1)
         out.yb_own(3)
         out.za_relay(1, 2, 1)
         out.za_relay(-1, 2, 1)
-        x_relay(1)
-        x_relay(-1)
         qkv.yb_relay(3, 1)
         qkv.yb_relay(3, -1)
-        qkv.za_relay(1, 3, 0)
         x_fin()
         layer_norm(0, 1)
         layer_norm(1, 1)
+        qkv.za_relay(1, 3, 0)
         layer_norm(2, 1)
         layer_norm(3, 1)
-        qkv.yb_relay(4, 1)
-        qkv.yb_relay(4, -1)
-        qkv.za_relay(-1, 3, 1)
         qkv.fin(0)
         qkv.fin(-1)
         qkv.fin(1)
         qkv.fin(-2)
         project((0, -1, 1, -2), True)
+        qkv.yb_relay(4, 1)
+        qkv.yb_relay(4, -1)
+        qkv.za_relay(-1, 3, 1)
         out.yb_relay(-3, 1)
         out.yb_relay(-3, -1)
-        out.yb_relay(3, 1)
-        out.yb_relay(3, -1)
         out.yb_own(4)
-        out.za_relay(1, 3, 0)
         qkv.fin(2)
         qkv.fin(-3)
         project((2, -3), False)
+        out.yb_relay(3, 1)
+        out.yb_relay(3, -1)
+        out.za_relay(1, 3, 0)
         out.za_relay(-1, 3, 1)
         out.yb_relay(4, 1)
         out.yb_relay(4, -1)
@@ -922,7 +929,6 @@
         out.fin(3)
         out.fin(4)
         reduce_and_finish()
-        result_ref[...] = res[...]
         for copy in links.started:
             copy.wait_send()
 

time: 126 us -> 126 us (level)
  no operation moved by 1% of the time
where the time goes in v5:
time: 126 us
  Pallas kernels  122 us (97%)
  local copies, waits for them, and re-layouts  3.62 us (3%)
    pallas_call x1, Pallas kernels, shards(): pl.pallas_call(kernel, out_shape=jax.ShapeDtypeStruct((SLOT, CW), BF16),...  122 us

profile of v5, /device:TPU:1, one launch (start us, length us, event | category | flops | bytes accessed | tf_op | source)
XLA Modules:
  0.0 125.9 jit_solution(7595863950468558371)
XLA Ops:
  0.7 0.7 pad_bitcast_fusion
  1.4 0.6 broadcast_in_dim.19.marks_ref
  2.0 0.6 broadcast_in_dim.8.feats_ref
  2.6 121.5 %patch_layers.1 = bf16[256,768]{1,0:T(8,128)(2,1)} custom-call(s32[1,4]{1,0:T(1,128)} %ends_ref.1, bf16[16,256]{1,0:T(8,128)(2,1)} %broadcast_in_dim.8.feats_ref, s32[8,128]{1,0:T(8,128)} %broadcast_in_dim.19.marks_ref, bf16[256,768]{1,0:T(8,128)(2,1)} %bitcast.19, bf16[3,256,3072]{2,1,0:T(8,128)(2,1)} %bitcast.16, bf16[3,96,768]{2,1,0:T(8,128)(2,1)} %bitcast.18, ...), custom_call_target="tpu_custom_call" | custom-call | tf_op jit(solution)/shard_map/patch_layers/pallas_call | solution.py:947
  124.1 1.8 %copy.11 = bf16[1,1,256,768]{3,2,1,0:T(8,128)(2,1)} copy(bf16[1,1,256,768]{3,2,1,0:T(8,128)(2,1)} %bitcast.17) | data formatting | bytes 786432
  (2 shorter events, 0.1 us)
